TPU v7x, 256 devices: a whole 4x4x8 slice. The times are simulated.
256 devices in a mesh: expert: 8 (over x, core), context: 32 (over y, z).
Axes of the slice: x: 4, y: 4, z: 8, core: 2. Of those that a mesh axis runs over, the one named last changes fastest.
Arguments:
- hidden: bfloat16 [8, 4096, 2048], P('expert', 'context'), may hold values from -6 to 6
- query: bfloat16 [8, 4096, 2048], P('expert', 'context'), may hold values from -120 to 120
- keys: bfloat16 [8, 4096, 512], P('expert', 'context'), may hold values from -6 to 6
- values: bfloat16 [8, 4096, 512], P('expert', 'context'), may hold values from -6 to 6
- x_inner: bfloat16 [8, 4096, 4096], P('expert', 'context'), may hold values from -6 to 6
- z_gate: bfloat16 [8, 4096, 4096], P('expert', 'context'), may hold values from -6 to 6
- dt_raw: bfloat16 [8, 4096, 4096], P('expert', 'context'), may hold values from -5 to 5
- b_proj: float32 [8, 4096, 16], P('expert', 'context'), may hold values from -0.6 to 0.6
- c_proj: float32 [8, 4096, 16], P('expert', 'context'), may hold values from -0.6 to 0.6
- conv_weight: float32 [4, 4096], replicated, may hold values from -3 to 3
- conv_bias: float32 [4096], replicated, may hold values from -3 to 3
- dt_bias: float32 [4096], replicated, may hold values from -0.5 to 0.5
- a_rate: float32 [16, 4096], replicated, may hold values from 7.324219e-05 to 0.05
- skip_gain: float32 [4096], replicated, may hold values from 0.5 to 1.5
- mamba_vector: float32 [4096], replicated, may hold values from -0.09375 to 0.09375
- attn_vector: float32 [2048], replicated, may hold values from -0.125 to 0.125
- impact_vector: float32 [2048], replicated, may hold values from -0.125 to 0.125
- norm_gain: float32 [2048], replicated, may hold values from 0.5 to 1.5
- expert_gate: bfloat16 [16, 2048, 7168], P('expert', None, 'context'), may hold values from -0.125 to 0.125
- expert_up: bfloat16 [16, 2048, 7168], P('expert', None, 'context'), may hold values from -0.125 to 0.125
- expert_vector: float32 [16, 7168], P('expert', 'context'), may hold values from -0.0625 to 0.0625
- routes: int32 [8, 4096, 2], P('expert', 'context'), may hold values from 0 to 15, all different within a row
- route_gate: float32 [8, 4096, 2], P('expert', 'context'), may hold values from 0.1 to 0.9
- lengths: int32 [8], replicated, may hold values from 1 to 4096, 20480 in all
- term_ids: int32 [8, 4096], P('expert', 'context'), may hold values from 0 to 65535
Outputs:
- token_impacts: float32 [8, 4096], P('expert', 'context')
- term_impacts: float32 [8, 65536], P('expert', 'context')
All inputs are finite; a program needn't handle non-finite values.
Results may differ from a plain program's by a relative error of at most 0.009.
Values may be sent and summed in bfloat16 or wider, within the bound.
A program may use at most 192 MiB of HBM per device.

v0:
```python
import jax
import jax.numpy as jnp
from jax import lax
from jax.sharding import PartitionSpec as P

H = 16
HD = 128
KVH = 4
KCONV = 4
VOCAB = 65536


big_negative = -1e30
norm_eps = 1e-06


def passed_along(x, axis, by):
    devices = lax.axis_size(axis)
    pairs = [(i, i + by) for i in range(devices) if 0 <= i + by < devices]
    return lax.ppermute(x, axis, pairs)


def prefix(x, axis, join, neutral):
    place = lax.axis_index(axis)
    gathered = jax.tree.map(
        lambda a, kind: lax.all_gather(a.astype(kind), axis), x, (jnp.bfloat16, jnp.bfloat16)
    )
    state = jax.tree.map(lambda a, e: jnp.zeros_like(a) + jnp.asarray(e, a.dtype), x, neutral)

    def one(turn, state):
        return join(
            state,
            jax.tree.map(
                lambda a, own: lax.dynamic_index_in_dim(a, turn, 0, False).astype(own.dtype),
                gathered,
                x,
            ),
        )

    return lax.fori_loop(0, place, one, state)


def shards(
    hidden,
    query,
    keys,
    values,
    x_inner,
    z_gate,
    dt_raw,
    b_proj,
    c_proj,
    conv_weight,
    conv_bias,
    dt_bias,
    a_rate,
    skip_gain,
    mamba_vector,
    attn_vector,
    impact_vector,
    norm_gain,
    expert_gate,
    expert_up,
    expert_vector,
    routes,
    route_gate,
    lengths,
    term_ids,
):
    tokens_here = hidden.shape[1]
    doc_index = lax.axis_index("expert")
    shard_index = lax.axis_index("context")
    doc_length = lax.dynamic_index_in_dim(lengths, doc_index, 0, False)
    positions = shard_index * tokens_here + jnp.arange(tokens_here, dtype=jnp.int32)
    live_rows = positions < doc_length
    groups = H // KVH
    score_scale = HD ** (-0.5)
    queries = query[0].reshape(tokens_here, KVH, groups, HD)

    def key_block(carried, kv_block, first_key):
        running_max, running_sum, running_out = carried
        key_rows, value_rows = kv_block
        block_width = key_rows.shape[0]
        key_heads = key_rows.reshape(block_width, KVH, HD)
        value_heads = value_rows.reshape(block_width, KVH, HD)
        scores = (
            jnp.einsum("tgqd,rgd->gqtr", queries, key_heads, preferred_element_type=jnp.float32)
            * score_scale
        )
        key_positions = first_key + jnp.arange(block_width, dtype=jnp.int32)
        allowed = key_positions[None, :] <= positions[:, None]
        scores = jnp.where(allowed, scores, big_negative)
        new_max = jnp.maximum(running_max, jnp.max(scores, axis=-1))
        exp_scores = jnp.where(allowed, jnp.exp(scores - new_max[..., None]), 0.0)
        factor = jnp.exp(running_max - new_max)
        running_sum = running_sum * factor + jnp.sum(exp_scores, axis=-1)
        running_out = running_out * factor[..., None] + jnp.einsum(
            "gqtr,rgd->gqtd",
            exp_scores.astype(jnp.bfloat16),
            value_heads,
            preferred_element_type=jnp.float32,
        )
        return (new_max, running_sum, running_out)

    start_state = (
        jnp.full((KVH, groups, tokens_here), big_negative, jnp.float32),
        jnp.zeros((KVH, groups, tokens_here), jnp.float32),
        jnp.zeros((KVH, groups, tokens_here, HD), jnp.float32),
    )
    key_piece = lax.all_gather(keys[0], "context", axis=0, tiled=True)
    value_piece = lax.all_gather(values[0], "context", axis=0, tiled=True)
    piece_rows = key_piece.shape[0]
    block_rows = 512

    def one_block(inner_state, offset):
        kv_block = (
            lax.dynamic_slice_in_dim(key_piece, offset, block_rows, 0),
            lax.dynamic_slice_in_dim(value_piece, offset, block_rows, 0),
        )
        updated = key_block(inner_state, kv_block, offset)
        return (updated, None)

    offsets = jnp.arange(0, piece_rows, block_rows, dtype=jnp.int32)
    final_state = lax.scan(one_block, start_state, offsets)[0]
    running_sum = final_state[1]
    attended = final_state[2] / jnp.where(running_sum > 0.0, running_sum, 1.0)[..., None]
    attended = (
        jnp.transpose(attended, (2, 0, 1, 3)).reshape(tokens_here, H * HD).astype(jnp.bfloat16)
    )
    attn_score = jnp.sum(attended.astype(jnp.float32) * attn_vector[None, :], axis=-1)
    inner_rows = x_inner[0]
    conv_rim = passed_along(inner_rows[tokens_here - (KCONV - 1) :], "context", 1)
    extended = jnp.concatenate([conv_rim, inner_rows], axis=0).astype(jnp.float32)
    conv_sum = conv_bias[None, :]
    for tap_index in range(KCONV):
        conv_sum = (
            conv_sum
            + conv_weight[tap_index][None, :] * extended[tap_index : tap_index + tokens_here]
        )
    conved = jax.nn.silu(conv_sum)
    step_size = jax.nn.softplus(dt_raw[0].astype(jnp.float32) + dt_bias[None, :])
    neg_rate = -a_rate
    b_rows = b_proj[0]
    c_rows = c_proj[0]

    def emit_rows(carried, per_step):
        size_now, b_now, c_now, x_now = per_step
        carried = (
            jnp.exp(size_now[None, :] * neg_rate) * carried
            + (size_now * x_now)[None, :] * b_now[:, None]
        )
        return (carried, jnp.sum(c_now[:, None] * carried, axis=0))

    zero_state = jnp.zeros(a_rate.shape, jnp.float32)
    local_end, local_outputs = lax.scan(emit_rows, zero_state, (step_size, b_rows, c_rows, conved))
    cumulative = jnp.cumsum(step_size, axis=0)
    through = jnp.exp(neg_rate * cumulative[tokens_here - 1][None, :])

    def chain(earlier_part, later_part):
        return (earlier_part[0] * later_part[0], later_part[0] * earlier_part[1] + later_part[1])

    chain_out = prefix((through, local_end), "context", chain, (jnp.ones_like(through), zero_state))
    incoming = chain_out[1]
    row_group = 32
    group_count = tokens_here // row_group

    def carried_in(operands):
        cumulative_rows, c_group = operands
        decayed = jnp.exp(cumulative_rows[:, None, :] * neg_rate[None, :, :])
        return jnp.sum(c_group[:, :, None] * decayed * incoming[None, :, :], axis=1)

    correction = lax.map(
        carried_in,
        (
            cumulative.reshape(group_count, row_group, cumulative.shape[1]),
            c_rows.reshape(group_count, row_group, c_rows.shape[1]),
        ),
    )
    outputs = local_outputs + correction.reshape(tokens_here, cumulative.shape[1])
    mamba_out = (
        (outputs + skip_gain[None, :] * conved) * jax.nn.silu(z_gate[0].astype(jnp.float32))
    ).astype(jnp.bfloat16)
    mamba_score = jnp.sum(mamba_out.astype(jnp.float32) * mamba_vector[None, :], axis=-1)
    hidden_rows = hidden[0].astype(jnp.float32)
    mean_square = jnp.mean(hidden_rows * hidden_rows, axis=-1, keepdims=True)
    normed = (hidden_rows * lax.rsqrt(mean_square + norm_eps) * norm_gain[None, :]).astype(
        jnp.bfloat16
    )
    axis_experts = lax.axis_size("expert")
    local_experts = expert_gate.shape[0]
    all_experts = axis_experts * local_experts
    capacity = tokens_here * 5 // 64
    expert_ids = jnp.arange(all_experts, dtype=jnp.int32)
    route_rows = routes[0]
    matches = (route_rows[:, :, None] == expert_ids[None, None, :]).astype(jnp.int32)
    chosen = jnp.sum(matches, axis=1) * live_rows[:, None].astype(jnp.int32)
    before = jnp.cumsum(chosen, axis=0) - chosen
    slot_ids = jnp.arange(capacity, dtype=jnp.int32)
    placed = (chosen[:, :, None] == 1) & (before[:, :, None] == slot_ids[None, None, :])
    placed = placed.reshape(tokens_here, axis_experts, local_experts, capacity)
    outgoing = jnp.einsum(
        "tilc,td->licd", placed.astype(jnp.bfloat16), normed, preferred_element_type=jnp.float32
    ).astype(jnp.bfloat16)
    arrived = lax.all_to_all(outgoing, "expert", split_axis=1, concat_axis=1, tiled=True)
    slot_rows = arrived.reshape(local_experts, axis_experts * capacity, normed.shape[1])
    row_piece = lax.all_gather(slot_rows, "context", axis=1, tiled=True)
    gate_part = jnp.einsum(
        "lrd,ldf->lrf", row_piece, expert_gate, preferred_element_type=jnp.float32
    )
    up_part = jnp.einsum("lrd,ldf->lrf", row_piece, expert_up, preferred_element_type=jnp.float32)
    inner_units = (jax.nn.silu(gate_part) * up_part).astype(jnp.bfloat16)
    partial_terms = jnp.sum(inner_units.astype(jnp.float32) * expert_vector[:, None, :], axis=-1)
    slot_values = lax.psum_scatter(partial_terms, "context", scatter_dimension=1, tiled=True)
    returned = lax.all_to_all(
        slot_values.reshape(local_experts, axis_experts, capacity),
        "expert",
        split_axis=1,
        concat_axis=1,
        tiled=True,
    )
    per_expert = jnp.einsum(
        "tilc,lic->til", placed.astype(jnp.float32), returned, precision=lax.Precision.HIGHEST
    ).reshape(tokens_here, all_experts)
    gate_weights = jnp.sum(route_gate[0][:, :, None] * matches.astype(jnp.float32), axis=1)
    expert_score = jnp.sum(per_expert * gate_weights, axis=-1)
    base_score = jnp.sum(hidden_rows * impact_vector[None, :], axis=-1)
    score = base_score + attn_score + mamba_score + expert_score
    impacts = jnp.where(live_rows, jax.nn.relu(score), 0.0)
    shard_count = lax.axis_size("context")
    vocab_block = VOCAB // shard_count
    pooled = jnp.zeros((VOCAB,), jnp.float32).at[term_ids[0]].max(impacts)
    everything = lax.pmax(pooled.astype(jnp.bfloat16), "context").astype(pooled.dtype)
    own_block = lax.dynamic_slice_in_dim(everything, shard_index * vocab_block, vocab_block, 0)
    return (impacts[None, :], own_block[None, :])


def solution(mesh):
    placed = (
        P("expert", "context", None),
        P("expert", "context", None),
        P("expert", "context", None),
        P("expert", "context", None),
        P("expert", "context", None),
        P("expert", "context", None),
        P("expert", "context", None),
        P("expert", "context", None),
        P("expert", "context", None),
        P(),
        P(),
        P(),
        P(),
        P(),
        P(),
        P(),
        P(),
        P(),
        P("expert", None, "context"),
        P("expert", None, "context"),
        P("expert", "context"),
        P("expert", "context", None),
        P("expert", "context", None),
        P(),
        P("expert", "context"),
    )
    return jax.shard_map(
        shards,
        mesh=mesh,
        in_specs=placed,
        out_specs=(P("expert", "context"), P("expert", "context")),
        check_vma=False,
    )
```

profile of v0, /device:TPU:1, one launch (start us, length us, event | category | flops | bytes accessed | tf_op | source)
XLA Modules:
  0.0 1119.8 jit_solution(12694423566203048189)
XLA Ops:
  7.2 1.8 copy.75
  12.3 4.4 collective-permute-start
  16.7 3.8 compare_select_fusion
  20.5 4.7 reduce_window_sum.22
  29.8 2.7 divide_multiply_fusion
  32.5 441.6 %while.57 = (s32[]{:T(128)}, f32[16,4096]{1,0:T(8,128)S(1)}, f32[128,4096]{1,0:T(8,128)}, f32[128,4096]{1,0:T(8,128)}, f32[16,4096]{1,0:T(8,128)S(1)}, /*index=5...) while((s32[]{:T(128)}, f32[16,4096]{1,0:T(8,128)S(1)}, ...), condition=%wide.region_8.9_spmd.clone.clone, body=%wide.region_6.8_spmd.clone.sunk.clone | while | flops 458755 | bytes 934379 | solution.py:155
  477.5 1.8 fusion.36
  481.6 16.0 %all_to_all.10 = bf16[2,8,10,2048]{3,0,2,1:T(2,128)(2,1)S(1)} all-to-all(bf16[2,8,10,2048]{3,0,2,1:T(2,128)(2,1)S(1)} %copy.85), channel_id=1, replica_groups=mesh['expert'=8,'context'=32] {'expert'}, dimensions={1} | all-to-all | bytes 1310720 | tf_op jit(solution)/shard_map/all_to_all | solution.py:204
  500.2 122.3 %while.56 = (s32[]{:T(128)}, f32[4,4,128]{2,1,0:T(4,128)S(1)}, f32[4,4,128]{2,1,0:T(4,128)S(1)}, f32[4,4,128,128]{3,2,1,0:T(8,128)}, s32[8]{0:T(128)S(1)}, /*ind...) while((s32[]{:T(128)}, f32[4,4,128]{2,1,0:T(4,128)S(1)}, ...), condition=%wide.region_4.5_spmd.clone.clone, body=%wide.region_1.0_spmd.clone.sunk.clone | while | flops 551365248 | bytes 35525820 | solution.py:124
  505.5 2.8 fusion.97
  508.3 3.3 fusion.98
  511.7 2.5 fusion.100
  519.5 2.8 fusion.97
  522.3 3.3 fusion.98
  525.8 3.7 fusion.100
  532.2 1.8 constant_dynamic-slice_fusion.13
  534.8 2.8 fusion.97
  537.6 3.4 fusion.98
  541.1 3.7 fusion.100
  550.2 2.8 fusion.97
  553.0 3.3 fusion.98
  556.4 3.7 fusion.100
  565.4 2.8 fusion.97
  568.3 3.3 fusion.98
  572.0 3.7 fusion.100
  578.4 1.8 constant_dynamic-slice_fusion.13
  581.0 2.8 fusion.97
  583.9 3.4 fusion.98
  587.5 3.7 fusion.100
  596.5 2.8 fusion.97
  599.4 3.3 fusion.98
  602.8 3.7 fusion.100
  611.7 3.1 fusion.97
  614.9 3.7 fusion.98
  618.8 3.7 fusion.100
  622.5 2.3 multiply_reduce_fusion.4
  625.0 94.9 %all-gather.10.cloned.1.call-done = bf16[2,2560,2048]{2,1,0:T(8,128)(2,1)} async-done(((bf16[2,80,2048]{2,1,0:T(8,128)(2,1)}), bf16[2,2560,2048]{2,1,0:T(8,128)(2,1)}) %all-gather.10.cloned.1.call-update) | async-done | bytes 20971536 | tf_op jit(solution)/shard_map/all_gather | solution.py:206
  719.9 12.7 %fusion.66 = f32[2,2560,224]{1,2,0:T(8,128)} fusion(bf16[2,2560,2048]{2,1,0:T(8,128)(2,1)} %all-gather.10.cloned.1.call-done, bf16[2,2048,224]{1,2,0:T(8,128)(2,1)S(1)} %copy-done), kind=kOutput, calls=%fused_computation.119 | convolution fusion | flops 4697620480 | bytes 27394048 | tf_op jit(solution)/shard_map/lrd,ldf->lrf/dot_general | solution.py:207
  732.6 12.3 %multiply_reduce_fusion.2 = f32[2,2560]{1,0:T(2,128)S(1)} fusion(f32[2,224]{1,0:T(2,128)S(1)} %copy-done.22, bf16[2,2560,2048]{2,1,0:T(8,128)(2,1)} %all-gather.10.cloned.1.call-done, bf16[2,2048,224]{1,2,0:T(8,128)(2,1)} %param.52, f32[2,2560,224]{1,2,0:T(8,128)} %fusion.66), kind=kOutput, calls=%fused_computation.40 | convolution fusion | flops 4707937280 | bytes 27416320 | tf_op jit(solution)/shard_map/lrd,ldf->lrf/dot_general | solution.py:210
  746.5 18.8 %while.55 = (s32[]{:T(128)}, f32[4,32,4096]{2,1,0:T(8,128)}, f32[4,32,16]{1,0,2:T(4,128)S(1)}, f32[4,32,4096]{2,1,0:T(8,128)}, f32[16,4096]{1,0:T(8,128)S(1)}, /*index=5*/f32[16,4096]{1,0:T(8,128)S(1)}) while((s32[]{:T(128)}, f32[4,32,4096]{2,1,0:T(8,128)}, f32[4,32,16]{1,0,2:T(4,128)S(1)}, f32[4,32,4096]{2,1,0:T(8,128)}, ...), condition=%wide.region_14.15_spmd.clone, body=%wide.region_12.14_spmd.sunk.clone | while | flops 8257538 | bytes 3680845 | solution.py:172
  747.8 2.7 multiply_reduce_fusion.9
  752.4 2.7 multiply_reduce_fusion.9
  757.1 2.7 multiply_reduce_fusion.9
  761.8 2.7 multiply_reduce_fusion.9
  765.3 189.8 %reduce-scatter.4.cloned.1.call-done = f32[80,2]{1,0:T(8,128)} async-done(((f32[2560,2]{1,0:T(8,128)}), f32[80,2]{1,0:T(8,128)}) %reduce-scatter.4.cloned.1.call-update) | async-done | bytes 656
  956.7 10.0 all-to-all-start.1
  966.7 6.5 multiply_reduce_fusion.3
  977.4 134.3 %all-reduce.2.cloned.1.call-done = bf16[65536]{0:T(1024)(128)(2,1)} async-done(((bf16[65536]{0:T(1024)(128)(2,1)}), bf16[65536]{0:T(1024)(128)(2,1)}) %all-reduce.2.cloned.1.call-update) | async-done | bytes 131088 | tf_op jit(solution)/shard_map/pmax | solution.py:232
  (721 shorter events, 497.2 us)
Async XLA Ops:
  7.2 712.7 %copy-start = (bf16[2,2048,224]{1,2,0:T(8,128)(2,1)S(1)}, bf16[2,2048,224]{1,2,0:T(8,128)(2,1)}, u32[]{:S(2)}) copy-start(bf16[2,2048,224]{1,2,0:T(8,128)(2,1)} %param.51) | copy-start | bytes 5505028
  7.2 493.0 %all-gather.12.cloned.1.call-start = ((), (), s32[]{:S(2)}) async-start(), calls=%async_computation.5 | async-start | bytes 4325376 | tf_op jit(solution)/shard_map/all_gather | solution.py:110
  9.0 491.1 %all-gather.14.cloned.1.call-start = ((), (), s32[]{:S(2)}) async-start(), calls=%async_computation.6 | async-start | bytes 4325376 | tf_op jit(solution)/shard_map/all_gather | solution.py:111
  10.8 614.0 %all-gather.16.cloned.1.call-start = ((), (), s32[]{:S(2)}) async-start(), calls=%async_computation.7 | async-start | bytes 4325376 | tf_op jit(solution)/shard_map/all_gather | solution.py:26
  12.3 17.2 %collective-permute-start = (bf16[3,4096]{1,0:T(4,128)(2,1)}, bf16[3,4096]{1,0:T(4,128)(2,1)S(1)}, u32[]{:S(2)}, u32[]{:S(2)}) collective-permute-start(bf16[3,4096]{1,0:T(4,128)(2,1)} %slice_bitcast_fusion), channel_id=1, source_target_pairs={{0,1},{1,2},{2,3},{3,4},{4,5},{5,6},{6,7},{7,8},{8,9},{9,10},{10,1... | collective-permute-start | bytes 73736 | tf_op jit(solution)/shard_map/ppermute | solution.py:20
  20.4 5.7 copy-start.7
  20.4 7.5 copy-start.14
  20.4 8.3 copy-start.9
  20.4 9.0 copy-start.4
  26.1 3.6 copy-start.8
  26.9 597.9 %all-gather.18.cloned.1.call-start = ((), (), s32[]{:S(2)}) async-start(), calls=%async_computation.8 | async-start | bytes 4325376 | tf_op jit(solution)/shard_map/all_gather | solution.py:26
  29.8 2.7 copy-start.3
  32.5 442.4 %copy-start.17 = (s32[1,128,2]{1,2,0:T(2,128)S(1)}, s32[1,128,2]{1,2,0:T(2,128)}, u32[]{:S(2)}) copy-start(s32[1,128,2]{1,2,0:T(2,128)} %param.54) | copy-start | bytes 3076
  32.5 442.7 %copy-start.23 = (s32[8]{0:T(128)S(1)}, s32[8]{0:T(128)}, u32[]{:S(2)}) copy-start(s32[8]{0:T(128)} %param.56) | copy-start | bytes 100
  474.1 3.4 copy-start.12
  474.8 4.5 copy-start.21
  474.8 245.1 %all-gather.10.cloned.1.call-start = ((), (), s32[]{:S(2)}) async-start(), calls=%async_computation.3 | async-start | bytes 21626880 | tf_op jit(solution)/shard_map/all_gather | solution.py:206
  477.5 3.4 copy-start.15
  480.9 18.0 %copy-start.10 = (f32[1,128,16]{1,2,0:T(8,128)S(1)}, f32[1,128,16]{1,2,0:T(8,128)}, u32[]{:S(2)}) copy-start(f32[1,128,16]{1,2,0:T(8,128)} %param.41) | copy-start | bytes 24580
  480.9 18.1 %copy-start.6 = (bf16[1,128,2048]{2,1,0:T(8,128)(2,1)S(1)}, bf16[1,128,2048]{2,1,0:T(8,128)(2,1)}, u32[]{:S(2)}) copy-start(bf16[1,128,2048]{2,1,0:T(8,128)(2,1)} %param.34) | copy-start | bytes 1572868
  497.5 2.1 copy-start.20
  497.5 2.1 copy-start.24
  498.7 456.5 %reduce-scatter.4.cloned.1.call-start = ((), (), s32[]{:S(2)}) async-start(), calls=%async_computation.9 | async-start | bytes 1351680
  500.2 122.3 %copy-start.13 = (f32[2048]{0:T(1024)S(1)}, f32[2048]{0:T(1024)}, u32[]{:S(2)}) copy-start(f32[2048]{0:T(1024)} %param.48) | copy-start | bytes 24580
  508.3 3.5 copy-start.2
  522.3 3.4 copy-start.2
  537.6 3.5 copy-start.2
  553.0 3.4 copy-start.2
  568.3 3.7 copy-start.2
  583.9 3.6 copy-start.2
  599.4 3.4 copy-start.2
  614.9 3.9 copy-start.2
  625.0 107.6 %copy-start.22 = (f32[2,224]{1,0:T(2,128)S(1)}, f32[2,224]{1,0:T(2,128)}, u32[]{:S(2)}) copy-start(f32[2,224]{1,0:T(2,128)} %param.53) | copy-start | bytes 5380
  746.5 220.2 %copy-start.5 = (bf16[1,128,4096]{2,1,0:T(8,128)(2,1)S(1)}, bf16[1,128,4096]{2,1,0:T(8,128)(2,1)}, u32[]{:S(2)}) copy-start(bf16[1,128,4096]{2,1,0:T(8,128)(2,1)} %param.38) | copy-start | bytes 3145732
  746.5 220.2 %copy-start.11 = (f32[4096]{0:T(1024)S(1)}, f32[4096]{0:T(1024)}, u32[]{:S(2)}) copy-start(f32[4096]{0:T(1024)} %param.47) | copy-start | bytes 49156
  956.7 16.5 %all-to-all-start.1 = ((f32[2,8,10]{2,0,1:T(2,128)}), f32[2,8,10]{2,0,1:T(2,128)S(1)}, u32[]{:S(2)}, u32[]{:S(2)}) async-start(f32[2,8,10]{2,0,1:T(2,128)} %copy.87), calls=%async_computation.1 | async-start | bytes 16384 | tf_op jit(solution)/shard_map/all_to_all | solution.py:214
  966.7 145.0 %all-reduce.2.cloned.1.call-start = ((), (), s32[]{:S(2)}) async-start(), calls=%async_computation.4 | async-start | bytes 262144 | tf_op jit(solution)/shard_map/pmax | solution.py:232
  966.7 6.5 copy-start.16
  966.7 6.7 copy-start.18
  966.7 6.7 copy-start.19
  966.7 146.2 %copy-start.1 = (bf16[2,2048,224]{1,2,0:T(8,128)(2,1)S(1)}, bf16[2,2048,224]{1,2,0:T(8,128)(2,1)}, u32[]{:S(2)}) copy-start(bf16[2,2048,224]{1,2,0:T(8,128)(2,1)} %param.51) | copy-start | bytes 5505028
Sparse Core Ops, SparseCore 0:
  10.5 83.8 all-gather.11
  96.8 83.3 all-gather.13
  182.8 82.4 all-gather.15
  475.0 81.5 all-gather.17
  559.0 160.8 all-gather.9
  746.6 208.4 reduce-scatter.3
  976.4 135.2 all-reduce.1
where the time goes:
time: 1130 us; the launch traced here: 1120 us
  waiting for transfers between devices  419 us (37%)
  local copies, waits for them, and re-layouts  340 us (30%)
  other arithmetic  220 us (19%)
  matrix products  78.1 us (7%)
  loops' own time  17.7 us (2%)
  blocking collectives  16 us (1%)
  starting transfers between devices  14.8 us (1%)
  between operations  14.6 us (1%)
    dynamic_update_slice x128, local copies, waits for them, and re-layouts, shards(): lax.scan(emit_rows, zero_state, (step_size, b_rows, c_rows, conved))  207 us
    unnamed x8, waiting for transfers between devices  190 us
    pmax x1, waiting for transfers between devices, shards(): lax.pmax(pooled.astype(jnp.bfloat16), 'context').astype(pooled.dtype)  134 us
    dynamic_slice x128, other arithmetic, shards(): lax.scan(emit_rows, zero_state, (step_size, b_rows, c_rows, conved))  128 us
    all_gather x1, waiting for transfers between devices, shards(): row_piece = lax.all_gather(slot_rows, 'context', axis=1, tiled=True)  94.9 us
    mul x128, local copies, waits for them, and re-layouts, emit_rows(): (size_now * x_now)[None, :] * b_now[:, None]  89 us
    dot_general x8, matrix products, key_block(): jnp.einsum('gqtr,rgd->gqtd', exp_scores.astype(jnp.bfloat16), value_heads...  28.6 us
    reduce_sum x8, other arithmetic, key_block(): running_sum = running_sum * factor + jnp.sum(exp_scores, axis=-1)  27.1 us
  transfers between devices with their start and end apart: 9, of which 3 were waited for; matrix products, arithmetic and copies ran while one was open for 54% of the time, Pallas kernels for 0%

commit v1 on v0

v1 whole, which is shorter than its diff:
```python
import jax
import jax.numpy as jnp
from jax import lax
from jax.experimental import pallas as pl
from jax.experimental.pallas import tpu as pltpu
from jax.sharding import PartitionSpec as P

H = 16
HD = 128
KVH = 4
GROUPS = H // KVH
KCONV = 4
VOCAB = 65536
D = 2048
INNER = 4096
NSTATE = 16
TOK = 128
CAP = 10
NE = 8
NCTX = 32
NY = 4
NZ = 8
FFL = 224
BLK = 512
NBLK = INNER // BLK
ROWS = NE * CAP
LOG2E = 1.4426950408889634
MESH = pl.DeviceIdType.MESH
F32 = jnp.float32
BF16 = jnp.bfloat16

NEG = -1e30
norm_eps = 1e-06


def iota(shape, axis):
    return lax.broadcasted_iota(jnp.int32, shape, axis)


def dot(a, b):
    return lax.dot_general(a, b, (((1,), (0,)), ((), ())), preferred_element_type=F32)


def dot_t(a, b):
    return lax.dot_general(a, b, (((1,), (1,)), ((), ())), preferred_element_type=F32)


def remote(src, dst, send, recv, device):
    return pltpu.make_async_remote_copy(
        src_ref=src, dst_ref=dst, send_sem=send, recv_sem=recv,
        device_id=device, device_id_type=MESH,
    )


def lane_sum(x):
    total = x[:, 0:128]
    for i in range(1, x.shape[1] // 128):
        total = total + x[:, 128 * i : 128 * (i + 1)]
    return total


def to_row(col):
    n = col.shape[0]
    eye = iota((n, 128), 0) == iota((n, 128), 1)
    return jnp.sum(jnp.where(eye, col, 0.0), axis=0, keepdims=True)


def to_col(row):
    eye = iota((128, 128), 0) == iota((128, 128), 1)
    return jnp.sum(jnp.where(eye, row, 0.0), axis=1, keepdims=True)


def kernel(
    hidden_ref, query_ref, keys_ref, values_ref, x_ref, z_ref, dtraw_ref, c_ref, a_ref,
    small_ref, ids_ref, chan_ref, feat_ref, vec_ref, w_ref,
    imp_ref, term_ref,
    wb, kb, rb, og, ar, dts, us, cvs, ext, rim, bexp, cbd, hb, pe, pr, ic, ir,
    qs, acc, ms, ls, vb, ma, zs, zr, es, er, imps, idb, lot, macc, base_s,
    lsem, ws, wr, ks, kr, vs, vr, zks, zkr, rs, rr, as_, ar_, ms_, mr_, ps, prs, qs_, qr_,
    z2s, z2r, e2s, e2r, i2s, i2r, d2s, d2r,
):
    e = lax.axis_index("expert")
    c = lax.axis_index("context")
    y = c // NZ
    z = c % NZ

    def ctx(yy, zz):
        return {"context": ((yy + NY) % NY) * NZ + (zz + NZ) % NZ}

    def cpeer(i):
        return {"context": (c + i) % NCTX}

    def epeer(i):
        return {"expert": (e + i) % NE}

    bar = pltpu.get_barrier_semaphore()

    @pl.loop(1, NCTX)
    def _(i):
        pl.semaphore_signal(bar, inc=1, device_id=cpeer(i), device_id_type=MESH)

    @pl.loop(1, NE)
    def _(i):
        pl.semaphore_signal(bar, inc=1, device_id=epeer(i), device_id_type=MESH)

    l0 = pltpu.make_async_copy(keys_ref, kb.at[z, y, :, 0:512], lsem.at[0])
    l1 = pltpu.make_async_copy(values_ref, kb.at[z, y, :, 512:1024], lsem.at[1])
    l2 = pltpu.make_async_copy(w_ref, wb.at[y], lsem.at[2])
    l0.start()
    l1.start()
    l2.start()

    hid = hidden_ref[...].astype(F32)
    mean_square = jnp.mean(hid * hid, axis=-1, keepdims=True)
    normed = (hid * lax.rsqrt(mean_square + norm_eps) * feat_ref[2:3, :]).astype(BF16)
    base_s[...] = jnp.broadcast_to(
        jnp.sum(hid * feat_ref[1:2, :], axis=-1, keepdims=True), (TOK, 128)
    )

    def routing():
        eio = iota((16, TOK), 0).astype(F32)
        m0 = small_ref[16:17, :] == eio
        m1 = small_ref[17:18, :] == eio
        live = small_ref[20:21, :]
        chosen = jnp.where(m0 | m1, live, 0.0)
        upper = jnp.where(iota((TOK, TOK), 0) < iota((TOK, TOK), 1), 1.0, 0.0).astype(BF16)
        before = dot(chosen.astype(BF16), upper)
        gates = jnp.where(m0, small_ref[18:19, :], 0.0) + jnp.where(m1, small_ref[19:20, :], 0.0)
        return chosen, before, gates

    chosen, before, _ = routing()
    sio = iota((16, TOK), 0)
    pieces = []
    for k in range(16):
        ok = (chosen[k : k + 1, :] == 1.0) & (before[k : k + 1, :] == sio.astype(F32)) & (sio < CAP)
        pieces.append(jnp.where(ok, 1.0, 0.0))
    placed = jnp.concatenate(pieces, axis=0).astype(BF16)
    og[...] = dot(placed, normed).astype(BF16).reshape(NE, 32, D)

    pl.semaphore_wait(bar, NCTX - 1 + NE - 1)
    l0.wait()
    l1.wait()
    kv_y = [remote(kb.at[z, y], kb.at[z, y], ks.at[i], kr.at[i], ctx(y + i + 1, z)) for i in range(3)]
    for k in kv_y:
        k.start()
    rim_copy = remote(x_ref.at[TOK - 16 : TOK], rim, ms_, mr_, {"context": (c + 1) % NCTX})
    rim_copy.start()

    def a2a(i):
        return remote(og.at[(e + i) % NE], ar.at[e], as_.at[i], ar_.at[i], epeer(i))

    @pl.loop(1, NE)
    def _(i):
        a2a(i).start()

    def ids_copy(i):
        return remote(ids_ref, idb.at[c], d2s.at[i], d2r.at[i], cpeer(i))

    vec_y = [remote(vec_ref, vb.at[y], vs.at[i], vr.at[i], ctx(y + i + 1, z)) for i in range(3)]
    for k in vec_y:
        k.start()
    ar[pl.ds(e, 1)] = og[pl.ds(e, 1)]
    vb[pl.ds(y, 1)] = vec_ref[...].reshape(1, 8, 512)
    idb[pl.ds(c, 1)] = ids_ref[...].reshape(1, 8, 128)

    for t in range(TOK):
        bexp[t] = jnp.broadcast_to(small_ref[0:16, t : t + 1], (16, 128))
    cf = c_ref[...]
    c_hi = cf.astype(BF16)
    c_lo = (cf - c_hi.astype(F32)).astype(BF16)
    rep = jnp.where(iota((16, 256), 0) == iota((16, 256), 1) % 16, 1.0, 0.0).astype(BF16)
    keep = (iota((TOK, 256), 1) // 16) == (iota((TOK, 256), 0) % 16)
    t_hi = jnp.where(keep, dot(c_hi, rep), 0.0).astype(BF16).reshape(8, 16, 256)
    t_lo = jnp.where(keep, dot(c_lo, rep), 0.0).astype(BF16).reshape(8, 16, 256)
    cbd[:, 0:16, :] = t_hi
    cbd[:, 16:32, :] = t_lo

    for g in range(KVH):
        for j in range(GROUPS):
            h = g * GROUPS + j
            qs[g, j * TOK : (j + 1) * TOK, :] = query_ref[:, h * HD : (h + 1) * HD]
    acc[...] = jnp.zeros_like(acc)
    ls[...] = jnp.zeros_like(ls)
    ms[...] = jnp.full_like(ms, NEG)
    ma[...] = jnp.zeros_like(ma)
    macc[...] = jnp.zeros_like(macc)
    zs[...] = jnp.zeros_like(zs)

    def zstep(buf, ss, rr_, s, half):
        bp = (z - (s - 1) + NZ) % NZ
        bm = (z + (s - 1)) % NZ
        if s < 4:
            return (
                remote(buf.at[bp], buf.at[bp], ss.at[0, s - 1], rr_.at[0, s - 1], ctx(y, z + 1)),
                remote(buf.at[bm], buf.at[bm], ss.at[1, s - 1], rr_.at[1, s - 1], ctx(y, z - 1)),
            )
        p = buf.at[bp, 0:half]
        m = buf.at[bm, half : 2 * half]
        return (
            remote(p, p, ss.at[0, s - 1], rr_.at[0, s - 1], ctx(y, z + 1)),
            remote(m, m, ss.at[1, s - 1], rr_.at[1, s - 1], ctx(y, z - 1)),
        )

    kv_step = [None] + [zstep(kb, zks, zkr, s, NY // 2) for s in range(1, 5)]
    row_step = [None] + [zstep(rb, rs, rr, s, ROWS) for s in range(1, 5)]

    def start(pair):
        for q in pair:
            q.start()

    def wait(pair):
        for q in pair:
            q.wait()

    w1 = (
        remote(wb.at[y], wb.at[y], ws.at[0], wr.at[0], ctx(y + 1, z)),
        remote(wb.at[y], wb.at[y], ws.at[1], wr.at[1], ctx(y - 1, z)),
    )
    ym = (y + NY - 1) % NY
    yp = (y + 1) % NY
    w2 = (
        remote(wb.at[ym, 0 : D // 2], wb.at[ym, 0 : D // 2], ws.at[2], wr.at[2], ctx(y + 1, z)),
        remote(wb.at[yp, D // 2 : D], wb.at[yp, D // 2 : D], ws.at[3], wr.at[3], ctx(y - 1, z)),
    )

    @pl.loop(1, NE)
    def _(i):
        a2a(i).wait()

    dst = iota((2 * ROWS, 256), 0)
    src = iota((2 * ROWS, 256), 1)
    dl, di, ds = dst // ROWS, (dst % ROWS) // CAP, dst % CAP
    pick = jnp.where(src == di * 32 + dl * 16 + ds, 1.0, 0.0).astype(BF16)
    rb[pl.ds(z, 1)] = dot(pick, ar[...].reshape(256, D)).astype(BF16).reshape(1, 2 * ROWS, D)
    start(row_step[1])
    wait(kv_y)
    start(kv_step[1])
    l2.wait()
    start(w1)

    @pl.loop(1, NCTX)
    def _(i):
        ids_copy(i).start()

    rim_copy.wait()

    @pl.loop(0, NBLK)
    def _(k):
        cols = pl.ds(pl.multiple_of(k * BLK, BLK), BLK)
        edge = jnp.where(c == 0, 0.0, rim[:, cols].astype(F32))
        ext[0:8, :] = edge[8:16, :]
        ext[8 : 8 + TOK, :] = x_ref[:, cols].astype(F32)
        for r in range(0, TOK, 32):
            rows = slice(r, r + 32)
            s = chan_ref[4:5, cols]
            for j in range(KCONV):
                s = s + chan_ref[j : j + 1, cols] * ext[r + 5 + j : r + 37 + j, :]
            cv = s / (1.0 + jnp.exp(-s))
            raw = dtraw_ref[rows, cols].astype(F32) + chan_ref[5:6, cols]
            step = jnp.maximum(raw, 0.0) + jnp.log1p(jnp.exp(-jnp.abs(raw)))
            cvs[rows, cols] = cv
            dts[rows, cols] = step
            us[rows, cols] = step * cv
        a2 = a_ref[:, cols] * (-LOG2E)

        def group(g, carried):
            h, total = carried
            base = pl.multiple_of(g * 16, 16)
            d16 = dts[pl.ds(base, 16), cols]
            u16 = us[pl.ds(base, 16), cols]
            for tt in range(16):
                b = jnp.concatenate([bexp[base + tt]] * (BLK // 128), axis=1)
                decay = jnp.exp2(a2 * d16[tt : tt + 1, :])
                h = decay * h + b * u16[tt : tt + 1, :]
            return h, total + jnp.sum(d16, axis=0, keepdims=True)

        h, total = lax.fori_loop(
            0, TOK // 16, group, (jnp.zeros((NSTATE, BLK), F32), jnp.zeros((1, BLK), F32))
        )
        for i in range(BLK // 128):
            part = jnp.concatenate(
                [h[:, 128 * i : 128 * i + 128],
                 jnp.broadcast_to(total[:, 128 * i : 128 * i + 128], (8, 128))],
                axis=0,
            )
            pe[pl.ds(k * (BLK // 128) + i, 1)] = part.reshape(1, 24, 128)

    def end_copy(i):
        return remote(pe.at[(c + i) % NCTX], pr.at[c], ps.at[i], prs.at[i], cpeer(i))

    @pl.loop(1, NCTX)
    def _(i):
        end_copy(i).start()

    pr[pl.ds(c, 1)] = pe[pl.ds(c, 1)]

    def attend(zz):
        key_pos = ((iota((TOK, 512), 1) // TOK) * NZ + zz) * TOK + iota((TOK, 512), 1) % TOK
        allowed = key_pos <= c * TOK + iota((TOK, 512), 0)
        bias = jnp.where(allowed, 0.0, NEG)

        @pl.loop(0, KVH)
        def _(g):
            kcol = pl.ds(pl.multiple_of(g * HD, HD), HD)
            vcol = pl.ds(pl.multiple_of(512 + g * HD, HD), HD)
            kk = kb[pl.ds(zz, 1), :, :, kcol].reshape(NY * TOK, HD)
            vv = kb[pl.ds(zz, 1), :, :, vcol].reshape(NY * TOK, HD)
            scores = dot_t(qs[g], kk)
            scores = (scores.reshape(GROUPS, TOK, 512) + bias[None]).reshape(GROUPS * TOK, 512)
            m_old = ms[g]
            m_new = jnp.maximum(m_old, jnp.max(scores, axis=-1, keepdims=True))
            scale = HD ** (-0.5) * LOG2E
            p = jnp.exp2((scores - jnp.concatenate([m_new] * 4, axis=1)) * scale)
            alpha = jnp.exp2((m_old - m_new) * scale)
            ls[g] = alpha * ls[g] + jnp.sum(p, axis=-1, keepdims=True)
            acc[g] = alpha * acc[g] + dot(p.astype(BF16), vv)
            ms[g] = m_new

    attend(z)

    @pl.loop(1, NCTX)
    def _(i):
        end_copy(i).wait()

    a2c = a_ref[:, pl.ds(pl.multiple_of(c * 128, 128), 128)] * (-LOG2E)

    def join(i, state):
        ic[pl.ds(i, 1)] = state.reshape(1, NSTATE, 128)
        part = pr[i]
        return jnp.exp2(a2c * part[16:17, :]) * state + part[0:16, :]

    lax.fori_loop(0, NCTX, join, jnp.zeros((NSTATE, 128), F32))

    def inc_copy(i):
        return remote(ic.at[(c + i) % NCTX], ir.at[c], qs_.at[i], qr_.at[i], cpeer(i))

    @pl.loop(1, NCTX)
    def _(i):
        inc_copy(i).start()

    ir[pl.ds(c, 1)] = ic[pl.ds(c, 1)]

    wait(row_step[1])
    start(row_step[2])
    wait(kv_step[1])
    start(kv_step[2])

    attend((z + 1) % NZ)
    attend((z + NZ - 1) % NZ)

    @pl.loop(1, NCTX)
    def _(i):
        inc_copy(i).wait()

    def second(lo, hi):
        @pl.loop(lo, hi)
        def _(k):
            cols = pl.ds(pl.multiple_of(k * BLK, BLK), BLK)
            a2 = a_ref[:, cols] * (-LOG2E)
            h0 = jnp.concatenate([ir[k * (BLK // 128) + i] for i in range(BLK // 128)], axis=1)

            def group(g, h):
                base = pl.multiple_of(g * 16, 16)
                rows = pl.ds(base, 16)
                d16 = dts[rows, cols]
                u16 = us[rows, cols]
                for tt in range(16):
                    b = jnp.concatenate([bexp[base + tt]] * (BLK // 128), axis=1)
                    decay = jnp.exp2(a2 * d16[tt : tt + 1, :])
                    h = decay * h + b * u16[tt : tt + 1, :]
                    hb[16 * tt : 16 * tt + 16, :] = h.astype(BF16)
                both = dot(cbd[g], hb[...])
                out = both[0:16, :] + both[16:32, :] + chan_ref[6:7, cols] * cvs[rows, cols]
                zg = z_ref[rows, cols].astype(F32)
                out = (out * (zg / (1.0 + jnp.exp(-zg)))).astype(BF16).astype(F32)
                macc[rows, :] += lane_sum(out * chan_ref[7:8, cols])
                return h

            lax.fori_loop(0, TOK // 16, group, h0)

    second(0, NBLK // 2)
    wait(row_step[2])
    start(row_step[3])
    second(NBLK // 2, NBLK)
    wait(kv_step[2])
    start(kv_step[3])
    attend((z + 2) % NZ)
    attend((z + NZ - 2) % NZ)

    wait(row_step[3])
    start(row_step[4])

    @pl.loop(1, NCTX)
    def _(i):
        ids_copy(i).wait()

    @pl.loop(0, NCTX)
    def _(i):
        row = idb[i][0:1, :]
        lot[pl.ds(i, 1)] = (
            jnp.where(jnp.bitwise_and(row, 127) == iota((128, 128), 0), 1.0, 0.0)
            .astype(BF16).reshape(1, 128, 128)
        )

    wait(w1)
    start(w2)
    wait(vec_y)
    wait(row_step[4])

    def experts(yb):
        for l in range(2):
            rows = rb[:, l * ROWS : (l + 1) * ROWS, :].reshape(NZ * ROWS, D)
            part = wb[pl.ds(yb, 1), :, l * 384 : l * 384 + 512].reshape(D, 512)
            both = dot(rows, part)
            up = pltpu.roll(both, 512 - FFL, 1)
            inner = ((both / (1.0 + jnp.exp(-both))) * up).astype(BF16).astype(F32)
            vec = vb[pl.ds(yb, 1)].reshape(8, 512)[l : l + 1, :]
            ma[l] += lane_sum(inner * vec)

    @pl.loop(0, 3)
    def _(i):
        experts((y + jnp.where(i == 2, NY - 1, i)) % NY)

    wait(kv_step[3])
    start(kv_step[4])
    attend((z + 3) % NZ)
    attend((z + NZ - 3) % NZ)

    wait(w2)
    experts((y + 2) % NY)

    for l in range(2):
        col = jnp.sum(ma[l], axis=1, keepdims=True)
        for q in range(NZ):
            zs[q, l : l + 1, :] = to_row(col[q * ROWS : (q + 1) * ROWS, :])

    def z_copy(i):
        return remote(zs.at[(z + i) % NZ], zr.at[z], z2s.at[i], z2r.at[i], ctx(y, z + i))

    @pl.loop(1, NZ)
    def _(i):
        z_copy(i).start()

    zr[pl.ds(z, 1)] = zs[pl.ds(z, 1)]
    wait(kv_step[4])
    attend((z + 4) % NZ)

    @pl.loop(1, NZ)
    def _(i):
        z_copy(i).wait()

    summed = zr[0]
    for q in range(1, NZ):
        summed = summed + zr[q]
    place = iota((16, 128), 0)
    es[...] = jnp.where(place == 2 * e, summed[0:1, :], 0.0) + jnp.where(
        place == 2 * e + 1, summed[1:2, :], 0.0
    )

    def e_copy(i):
        return remote(es, er.at[e], e2s.at[i], e2r.at[i], epeer(i))

    @pl.loop(1, NE)
    def _(i):
        e_copy(i).start()

    er[pl.ds(e, 1)] = es[...].reshape(1, 16, 128)

    attn = jnp.zeros((TOK, 128), F32)
    for g in range(KVH):
        ratio = (acc[g] / ls[g]).astype(BF16).astype(F32)
        for j in range(GROUPS):
            h = g * GROUPS + j
            attn = attn + ratio[j * TOK : (j + 1) * TOK, :] * feat_ref[0:1, h * HD : (h + 1) * HD]
    attn_col = jnp.sum(attn, axis=1, keepdims=True)
    mamba_col = jnp.sum(macc[...], axis=1, keepdims=True)
    own = to_row(base_s[:, 0:1] + attn_col + mamba_col)
    id_row = ids_ref[0:1, :].astype(F32)
    id_same = to_col(id_row) == id_row
    chosen, before, gates = routing()

    @pl.loop(1, NE)
    def _(i):
        e_copy(i).wait()

    back = er[0]
    for q in range(1, NE):
        back = back + er[q]
    value = jnp.zeros((16, TOK), F32)
    for s in range(CAP):
        one = jnp.sum(jnp.where(iota((16, 128), 1) == e * CAP + s, back, 0.0), axis=1, keepdims=True)
        value = value + jnp.where((chosen == 1.0) & (before == float(s)), one, 0.0)
    expert = jnp.sum(value * gates, axis=0, keepdims=True)
    impacts = small_ref[20:21, :] * jnp.maximum(own + expert, 0.0)
    imp_ref[...] = impacts

    imp_col = to_col(impacts)
    earlier = iota((TOK, TOK), 0) < iota((TOK, TOK), 1)
    beaten = id_same & ((imp_col > impacts) | ((imp_col == impacts) & earlier))
    beaten = jnp.max(jnp.where(beaten, 1.0, 0.0), axis=0, keepdims=True)
    sent = jnp.where(beaten > 0.0, 0.0, impacts)
    imps[pl.ds(c, 1)] = jnp.broadcast_to(sent, (8, 128)).reshape(1, 8, 128)

    def imp_copy(i):
        return remote(imps.at[c], imps.at[c], i2s.at[i], i2r.at[i], cpeer(i))

    @pl.loop(1, NCTX)
    def _(i):
        imp_copy(i).start()

    @pl.loop(1, NCTX)
    def _(i):
        imp_copy(i).wait()

    def pool(i, best):
        word = jnp.right_shift(idb[i][0:1, :], 7) - c * 16
        val = jnp.where(word == iota((16, 128), 0), imps[i][0:1, :], 0.0)
        p0 = val.astype(BF16)
        rest = val - p0.astype(F32)
        p1 = rest.astype(BF16)
        p2 = (rest - p1.astype(F32)).astype(BF16)
        got = dot_t(jnp.concatenate([p0, p1, p2], axis=0), lot[i])
        return jnp.maximum(best, (got[0:16] + got[16:32]) + got[32:48])

    best = lax.fori_loop(0, NCTX, pool, jnp.zeros((16, 128), F32))
    for r in range(16):
        term_ref[0:1, 128 * r : 128 * r + 128] = best[r : r + 1, :]


def shards(
    hidden, query, keys, values, x_inner, z_gate, dt_raw, b_proj, c_proj, conv_weight, conv_bias,
    dt_bias, a_rate, skip_gain, mamba_vector, attn_vector, impact_vector, norm_gain, expert_gate,
    expert_up, expert_vector, routes, route_gate, lengths, term_ids,
):
    e = lax.axis_index("expert")
    c = lax.axis_index("context")
    length = lax.dynamic_index_in_dim(lengths, e, 0, False)
    live = (c * TOK + jnp.arange(TOK, dtype=jnp.int32) < length).astype(F32)
    small = jnp.concatenate(
        [b_proj[0].T, routes[0].T.astype(F32), route_gate[0].T, live[None, :], jnp.zeros((3, TOK), F32)],
        axis=0,
    )
    ids = jnp.broadcast_to(term_ids, (8, TOK))
    chan = jnp.concatenate(
        [conv_weight, conv_bias[None], dt_bias[None], skip_gain[None], mamba_vector[None]], axis=0
    )
    feat = jnp.stack([attn_vector, impact_vector, norm_gain, norm_gain])
    weights = jnp.concatenate([expert_gate[0], expert_up[0], expert_gate[1], expert_up[1]], axis=1)
    vec = jnp.concatenate(
        [jnp.pad(expert_vector[0:1], ((0, 0), (0, 512 - FFL))),
         jnp.pad(expert_vector[1:2], ((0, 0), (64, 512 - FFL - 64))),
         jnp.zeros((6, 512), F32)],
        axis=0,
    )
    dma = pltpu.SemaphoreType.DMA
    vmem = pltpu.VMEM
    outs = pl.pallas_call(
        kernel,
        name="layers",
        out_shape=OUT_SHAPE,
        in_specs=[pl.BlockSpec(memory_space=pltpu.VMEM)] * 14 + [pl.BlockSpec(memory_space=pl.ANY)],
        out_specs=OUT_SPECS,
        scratch_shapes=[
            vmem((NY, D, 4 * FFL), BF16), vmem((NZ, NY, TOK, 1024), BF16), vmem((NZ, 2 * ROWS, D), BF16),
            vmem((NE, 32, D), BF16), vmem((NE, 32, D), BF16),
            vmem((TOK, INNER), F32), vmem((TOK, INNER), F32), vmem((TOK, INNER), F32),
            vmem((8 + TOK, BLK), F32), vmem((16, INNER), BF16), vmem((TOK, 16, 128), F32),
            vmem((8, 32, 256), BF16), vmem((256, BLK), BF16),
            vmem((NCTX, 24, 128), F32), vmem((NCTX, 24, 128), F32),
            vmem((NCTX, 16, 128), F32), vmem((NCTX, 16, 128), F32),
            vmem((KVH, GROUPS * TOK, HD), BF16), vmem((KVH, GROUPS * TOK, HD), F32),
            vmem((KVH, GROUPS * TOK, 128), F32), vmem((KVH, GROUPS * TOK, 128), F32),
            vmem((NY, 8, 512), F32), vmem((2, NZ * ROWS, 128), F32),
            vmem((NZ, 8, 128), F32), vmem((NZ, 8, 128), F32),
            vmem((16, 128), F32), vmem((NE, 16, 128), F32),
            vmem((NCTX, 8, 128), F32), vmem((NCTX, 8, 128), jnp.int32), vmem((NCTX, 128, 128), BF16),
            vmem((TOK, 128), F32), vmem((TOK, 128), F32),
            dma((3,)), dma((4,)), dma((4,)), dma((3,)), dma((3,)), dma((3,)), dma((3,)),
            dma((2, 4)), dma((2, 4)), dma((2, 4)), dma((2, 4)), dma((NE,)), dma((NE,)), dma, dma,
            dma((NCTX,)), dma((NCTX,)), dma((NCTX,)), dma((NCTX,)),
            dma((NZ,)), dma((NZ,)), dma((NE,)), dma((NE,)), dma((NCTX,)), dma((NCTX,)),
            dma((NCTX,)), dma((NCTX,)),
        ],
        compiler_params=pltpu.CompilerParams(
            collective_id=0, has_side_effects=True, vmem_limit_bytes=VMEM_LIMIT
        ),
    )(
        hidden[0], query[0], keys[0], values[0], x_inner[0], z_gate[0], dt_raw[0], c_proj[0], a_rate,
        small, ids, chan, feat, vec, weights,
    )
    return tuple(outs)


OUT_SHAPE = (jax.ShapeDtypeStruct((1, TOK), F32), jax.ShapeDtypeStruct((1, VOCAB // NCTX), F32))
OUT_SPECS = (pl.BlockSpec(memory_space=pltpu.VMEM),) * 2
VMEM_LIMIT = 63 << 20


def solution(mesh):
    doc = P("expert", "context", None)
    placed = (doc,) * 9 + (P(),) * 9 + (
        P("expert", None, "context"),
        P("expert", None, "context"),
        P("expert", "context"),
        doc,
        doc,
        P(),
        P("expert", "context"),
    )
    return jax.shard_map(
        shards,
        mesh=mesh,
        in_specs=placed,
        out_specs=(P("expert", "context"), P("expert", "context")),
        check_vma=False,
    )
```

time: 1130 us -> 275 us (0.24)
  waiting for transfers between devices: 419 us -> 0 us
  local copies, waits for them, and re-layouts: 340 us -> 18.3 us
  Pallas kernels: 0 us -> 247 us
  other arithmetic: 220 us -> 7.91 us
  matrix products: 78.1 us -> 0 us
  loops' own time: 17.7 us -> 0 us
  blocking collectives: 16 us -> 0 us
  starting transfers between devices: 14.8 us -> 0 us
  between operations: 14.6 us -> 0.76 us
    pallas_call x0 -> x1, Pallas kernels: none -> 247 us  [shards(): pl.pallas_call(kernel, name='layers', out_shape=OUT_SHAPE, in_specs=[pl.B...]
    dynamic_update_slice x132 -> x0, local copies, waits for them, and re-layouts: 210 us -> none  [the longest x128 207 us: shards(): lax.scan(emit_rows, zero_state, (step_size, b_rows, c_rows, conved))]
    unnamed x8 -> x0, waiting for transfers between devices: 190 us -> none
    pmax x1 -> x0, waiting for transfers between devices: 134 us -> none  [shards(): lax.pmax(pooled.astype(jnp.bfloat16), 'context').astype(pooled.dtype)]
    dynamic_slice x128 -> x0, other arithmetic: 128 us -> none  [shards(): lax.scan(emit_rows, zero_state, (step_size, b_rows, c_rows, conved))]
    all_gather x5 -> x0, waiting for transfers between devices: 94.9 us -> none  [the longest x1 94.9 us: shards(): row_piece = lax.all_gather(slot_rows, 'context', axis=1, tiled=True)]
    mul x136 -> x0, local copies, waits for them, and re-layouts: 93.7 us -> none  [the longest x128 89 us: emit_rows(): (size_now * x_now)[None, :] * b_now[:, None]]
    dot_general x20 -> x0, matrix products: 78.1 us -> none  [the longest x8 28.6 us: key_block(): jnp.einsum('gqtr,rgd->gqtd', exp_scores.astype(jnp.bfloat16), value_heads...]
  transfers between devices with their start and end apart: 9 -> 0, of which waited for: 3 -> 0; matrix products, arithmetic and copies ran while one was open for 54% -> 0% of each run, Pallas kernels for 0% -> 0%
where the time goes in v1:
time: 275 us; the launch traced here: 274 us
  Pallas kernels  247 us (90%)
  local copies, waits for them, and re-layouts  18.3 us (7%)
  other arithmetic  7.91 us (3%)
    pallas_call x1, Pallas kernels, shards(): pl.pallas_call(kernel, name='layers', out_shape=OUT_SHAPE, in_specs=[pl.B...  247 us
    unnamed x29, local copies, waits for them, and re-layouts  7.93 us

profile of v1, /device:TPU:1, one launch (start us, length us, event | category | flops | bytes accessed | tf_op | source)
XLA Modules:
  0.0 274.4 jit_solution(8144329849913947253)
XLA Ops:
  0.6 1.2 dynamic_slice.4
  1.9 0.6 compare_convert_fusion
  2.5 0.7 convert_bitcast_fusion
  3.2 2.6 concatenate.12.small_ref
  5.8 2.6 fusion.2
  8.4 0.5 copy.32
  8.9 2.6 fusion.3
  11.5 0.5 copy.33
  12.0 1.5 copy.34
  13.5 2.3 copy.35
  15.7 0.0 copy-start.9
  15.7 0.0 copy-start
  15.7 0.0 copy-start.1
  15.7 0.0 copy-start.2
  15.7 0.0 copy-start.3
  15.7 0.0 copy-start.4
  15.7 0.0 copy-start.5
  15.8 0.0 copy-start.6
  15.8 0.0 copy-start.7
  15.8 0.0 copy-start.8
  15.8 0.0 copy-start.10
  15.8 5.3 %pad_maximum_fusion.w_ref = bf16[2048,896]{1,0:T(8,128)(2,1)} fusion(bf16[2048,224]{1,0:T(8,128)(2,1)} %bitcast.34, bf16[2048,224]{1,0:T(8,128)(2,1)S(1)} %bitcast.33, bf16[2048,224]{1,0:T(8,128)(2,1)S(1)} %bitcast.32, bf16[2048,224]{1,0:T(8,128)(2,1)S(1)} %bitcast.31), kind=kLoop, calls=%fused_computation | loop fusion | flops 14680064 | bytes 7340032 | tf_op jit(solution)/shard_map/concatenate | solution.py:548
  21.1 0.0 copy-done.9
  21.1 0.1 pad.16.clone
  21.2 0.7 fusion.vec_ref
  21.8 0.0 copy-done
  21.8 0.0 copy-done.1
  21.8 0.0 copy-done.2
  21.8 0.0 copy-done.3
  21.8 0.0 copy-done.4
  21.9 0.8 concatenate.13.chan_ref
  22.6 0.0 copy-done.5
  22.6 0.7 copy.27
  23.4 0.0 copy-done.6
  23.4 0.0 copy-done.7
  23.4 0.0 copy-done.8
  23.4 0.6 pad_maximum_fusion.1.feat_ref
  24.0 0.0 copy-done.10
  24.0 0.6 broadcast_in_dim.28.ids_ref
  24.6 247.4 %layers.1 = (f32[1,128]{1,0:T(1,128)}, f32[1,2048]{1,0:T(1,128)}) custom-call(bf16[128,2048]{1,0:T(8,128)(2,1)} %bitcast.38, bf16[128,2048]{1,0:T(8,128)(2,1)} %bitcast.39, bf16[128,512]{1,0:T(8,128)(2,1)} %bitcast.41, bf16[128,512]{1,0:T(8,128)(2,1)} %bitcast.42, bf16[128,4096]{1,0:T(8,128)(2,1)} %bitcast.35, bf16[128,4096]{1,0:T(8,128)(2,1)} %bitcast.36, ...), custom_call_target="tpu_custom_call" | custom-call | tf_op jit(solution)/shard_map/layers/pallas_call | solution.py:557
  272.0 1.1 copy.38
  273.1 1.3 copy.39
  (3 shorter events, 0.0 us)
Async XLA Ops:
  15.7 5.4 %copy-start.9 = (f32[2,224]{1,0:T(2,128)S(1)}, f32[2,224]{1,0:T(2,128)}, u32[]{:S(2)}) copy-start(f32[2,224]{1,0:T(2,128)} %param.45) | copy-start | bytes 5380
  15.7 6.1 %copy-start = (f32[4,4096]{1,0:T(4,128)S(1)}, f32[4,4096]{1,0:T(4,128)}, u32[]{:S(2)}) copy-start(f32[4,4096]{1,0:T(4,128)} %param.34) | copy-start | bytes 196612
  15.7 6.1 %copy-start.1 = (f32[4096]{0:T(1024)S(1)}, f32[4096]{0:T(1024)}, u32[]{:S(2)}) copy-start(f32[4096]{0:T(1024)} %param.35) | copy-start | bytes 49156
  15.7 6.1 %copy-start.2 = (f32[4096]{0:T(1024)S(1)}, f32[4096]{0:T(1024)}, u32[]{:S(2)}) copy-start(f32[4096]{0:T(1024)} %param.36) | copy-start | bytes 49156
  15.7 6.1 %copy-start.3 = (f32[4096]{0:T(1024)S(1)}, f32[4096]{0:T(1024)}, u32[]{:S(2)}) copy-start(f32[4096]{0:T(1024)} %param.38) | copy-start | bytes 49156
  15.7 6.1 %copy-start.4 = (f32[4096]{0:T(1024)S(1)}, f32[4096]{0:T(1024)}, u32[]{:S(2)}) copy-start(f32[4096]{0:T(1024)} %param.39) | copy-start | bytes 49156
  15.7 6.9 %copy-start.5 = (f32[1,128,16]{1,2,0:T(8,128)S(1)}, f32[1,128,16]{1,2,0:T(8,128)}, u32[]{:S(2)}) copy-start(f32[1,128,16]{1,2,0:T(8,128)} %param.33) | copy-start | bytes 24580
  15.8 7.6 %copy-start.6 = (f32[2048]{0:T(1024)S(1)}, f32[2048]{0:T(1024)}, u32[]{:S(2)}) copy-start(f32[2048]{0:T(1024)} %param.42) | copy-start | bytes 24580
  15.8 7.6 %copy-start.7 = (f32[2048]{0:T(1024)S(1)}, f32[2048]{0:T(1024)}, u32[]{:S(2)}) copy-start(f32[2048]{0:T(1024)} %param.41) | copy-start | bytes 24580
  15.8 7.6 %copy-start.8 = (f32[2048]{0:T(1024)S(1)}, f32[2048]{0:T(1024)}, u32[]{:S(2)}) copy-start(f32[2048]{0:T(1024)} %param.40) | copy-start | bytes 24580
  15.8 8.2 %copy-start.10 = (s32[1,128]{1,0:T(1,128)S(1)}, s32[1,128]{1,0:T(1,128)}, u32[]{:S(2)}) copy-start(s32[1,128]{1,0:T(1,128)} %param.49) | copy-start | bytes 1540

commit v2 on v1

--- a/solution.py
+++ b/solution.py
@@ -45,6 +45,10 @@
     return lax.dot_general(a, b, (((1,), (1,)), ((), ())), preferred_element_type=F32)
 
 
+def dot_l(a, b):
+    return lax.dot_general(a, b, (((0,), (0,)), ((), ())), preferred_element_type=F32)
+
+
 def remote(src, dst, send, recv, device):
     return pltpu.make_async_remote_copy(
         src_ref=src, dst_ref=dst, send_sem=send, recv_sem=recv,
@@ -72,11 +76,12 @@
 
 def kernel(
     hidden_ref, query_ref, keys_ref, values_ref, x_ref, z_ref, dtraw_ref, c_ref, a_ref,
-    small_ref, ids_ref, chan_ref, feat_ref, vec_ref, w_ref,
+    b_ref, routes_ref, gates_ref, len_ref, terms_ref, taps_ref, cbias_ref, dbias_ref, skip_ref, mvec_ref,
+    avec_ref, ivec_ref, gain_ref, evec_ref, gate_ref, up_ref,
     imp_ref, term_ref,
     wb, kb, rb, og, ar, dts, us, cvs, ext, rim, bexp, cbd, hb, pe, pr, ic, ir,
     qs, acc, ms, ls, vb, ma, zs, zr, es, er, imps, idb, lot, macc, base_s,
-    lsem, ws, wr, ks, kr, vs, vr, zks, zkr, rs, rr, as_, ar_, ms_, mr_, ps, prs, qs_, qr_,
+    lsem, ws, wr, ks, kr, vs, vr, zos, zor, zks, zkr, rs, rr, as_, ar_, ms_, mr_, ps, prs, qs_, qr_,
     z2s, z2r, e2s, e2r, i2s, i2r, d2s, d2r,
 ):
     e = lax.axis_index("expert")
@@ -103,29 +108,113 @@
     def _(i):
         pl.semaphore_signal(bar, inc=1, device_id=epeer(i), device_id_type=MESH)
 
-    l0 = pltpu.make_async_copy(keys_ref, kb.at[z, y, :, 0:512], lsem.at[0])
-    l1 = pltpu.make_async_copy(values_ref, kb.at[z, y, :, 512:1024], lsem.at[1])
-    l2 = pltpu.make_async_copy(w_ref, wb.at[y], lsem.at[2])
+    l0 = pltpu.make_async_copy(keys_ref, kb.at[z, 0, :, 0:512], lsem.at[0])
+    l1 = pltpu.make_async_copy(values_ref, kb.at[z, 0, :, 512:1024], lsem.at[1])
+    load_w = []
+    for l in range(2):
+        at = 2 * FFL * l
+        load_w.append(pltpu.make_async_copy(gate_ref.at[l], wb.at[y, at : at + FFL], lsem.at[2 + 2 * l]))
+        at = at + FFL
+        load_w.append(pltpu.make_async_copy(up_ref.at[l], wb.at[y, at : at + FFL], lsem.at[3 + 2 * l]))
     l0.start()
     l1.start()
-    l2.start()
+    for k in load_w:
+        k.start()
+
+    def zstep(view, ss, rr_, s):
+        bp = (z - (s - 1) + NZ) % NZ
+        bm = (z + (s - 1)) % NZ
+        p, m = view(bp, 0 if s == 4 else None), view(bm, 1 if s == 4 else None)
+        return (
+            remote(p, p, ss.at[0, s - 1], rr_.at[0, s - 1], ctx(y, z + 1)),
+            remote(m, m, ss.at[1, s - 1], rr_.at[1, s - 1], ctx(y, z - 1)),
+        )
+
+    def own_view(b, half):
+        if half is None:
+            return kb.at[b, 0]
+        return kb.at[b, 0, half * 64 : half * 64 + 64]
+
+    def kv_view(b, half):
+        if half is None:
+            return kb.at[b, 1:NY]
+        return kb.at[b, 1:NY, half * 64 : half * 64 + 64]
+
+    def row_view(b, half):
+        if half is None:
+            return rb.at[b]
+        return rb.at[b, half * ROWS : (half + 1) * ROWS]
+
+    own_step = [None] + [zstep(own_view, zos, zor, s) for s in range(1, 5)]
+    kv_step = [None] + [zstep(kv_view, zks, zkr, s) for s in range(1, 5)]
+    row_step = [None] + [zstep(row_view, rs, rr, s) for s in range(1, 5)]
+
+    def start(pair):
+        for q in pair:
+            q.start()
+
+    def wait(pair):
+        for q in pair:
+            q.wait()
+
+    def w1(q):
+        own = wb.at[y, q * FFL : (q + 1) * FFL]
+        return (
+            remote(own, own, ws.at[0, q], wr.at[0, q], ctx(y + 1, z)),
+            remote(own, own, ws.at[1, q], wr.at[1, q], ctx(y - 1, z)),
+        )
+
+    ym = (y + NY - 1) % NY
+    yp = (y + 1) % NY
+    w2 = (
+        remote(wb.at[ym, 0 : 2 * FFL], wb.at[ym, 0 : 2 * FFL], ws.at[0, 4], wr.at[0, 4], ctx(y + 1, z)),
+        remote(wb.at[yp, 2 * FFL : 4 * FFL], wb.at[yp, 2 * FFL : 4 * FFL], ws.at[1, 4], wr.at[1, 4], ctx(y - 1, z)),
+    )
+
+    idb[pl.ds(c, 1)] = terms_ref[...].reshape(1, 1, TOK)
+    vb[pl.ds(y, 1), 0:2, :] = evec_ref[...].reshape(1, 2, FFL)
+    l0.wait()
+    l1.wait()
+    pl.semaphore_wait(bar, NCTX - 1 + NE - 1)
+    rim_copy = remote(x_ref.at[TOK - 16 : TOK], rim, ms_, mr_, {"context": (c + 1) % NCTX})
+    rim_copy.start()
+    vec_y = [remote(vb.at[y], vb.at[y], vs.at[i], vr.at[i], ctx(y + i + 1, z)) for i in range(3)]
+    start(own_step[1])
+    start(vec_y)
+    kv_y = [remote(kb.at[z, 0], kb.at[z, 3 - i], ks.at[i], kr.at[i], ctx(y + i + 1, z)) for i in range(3)]
+    start(kv_y)
+
+    def ids_copy(i):
+        return remote(idb.at[c], idb.at[c], d2s.at[i], d2r.at[i], cpeer(i))
+
+    @pl.loop(1, NCTX)
+    def _(i):
+        ids_copy(i).start()
+
+    wait(load_w)
+    start(w1(0))
+    start(w1(1))
 
     hid = hidden_ref[...].astype(F32)
     mean_square = jnp.mean(hid * hid, axis=-1, keepdims=True)
-    normed = (hid * lax.rsqrt(mean_square + norm_eps) * feat_ref[2:3, :]).astype(BF16)
+    normed = (hid * lax.rsqrt(mean_square + norm_eps) * gain_ref[...]).astype(BF16)
     base_s[...] = jnp.broadcast_to(
-        jnp.sum(hid * feat_ref[1:2, :], axis=-1, keepdims=True), (TOK, 128)
+        jnp.sum(hid * ivec_ref[...], axis=-1, keepdims=True), (TOK, 128)
     )
+
+    live = (c * TOK + iota((1, TOK), 1) < len_ref[e]).astype(F32)
+    r0, r1 = routes_ref[0:1, :].astype(F32), routes_ref[1:2, :].astype(F32)
+    g0, g1 = gates_ref[0:1, :], gates_ref[1:2, :]
+    b_rows = b_ref[...]
 
     def routing():
         eio = iota((16, TOK), 0).astype(F32)
-        m0 = small_ref[16:17, :] == eio
-        m1 = small_ref[17:18, :] == eio
-        live = small_ref[20:21, :]
+        m0 = r0 == eio
+        m1 = r1 == eio
         chosen = jnp.where(m0 | m1, live, 0.0)
         upper = jnp.where(iota((TOK, TOK), 0) < iota((TOK, TOK), 1), 1.0, 0.0).astype(BF16)
         before = dot(chosen.astype(BF16), upper)
-        gates = jnp.where(m0, small_ref[18:19, :], 0.0) + jnp.where(m1, small_ref[19:20, :], 0.0)
+        gates = jnp.where(m0, g0, 0.0) + jnp.where(m1, g1, 0.0)
         return chosen, before, gates
 
     chosen, before, _ = routing()
@@ -137,14 +226,6 @@
     placed = jnp.concatenate(pieces, axis=0).astype(BF16)
     og[...] = dot(placed, normed).astype(BF16).reshape(NE, 32, D)
 
-    pl.semaphore_wait(bar, NCTX - 1 + NE - 1)
-    l0.wait()
-    l1.wait()
-    kv_y = [remote(kb.at[z, y], kb.at[z, y], ks.at[i], kr.at[i], ctx(y + i + 1, z)) for i in range(3)]
-    for k in kv_y:
-        k.start()
-    rim_copy = remote(x_ref.at[TOK - 16 : TOK], rim, ms_, mr_, {"context": (c + 1) % NCTX})
-    rim_copy.start()
 
     def a2a(i):
         return remote(og.at[(e + i) % NE], ar.at[e], as_.at[i], ar_.at[i], epeer(i))
@@ -153,25 +234,17 @@
     def _(i):
         a2a(i).start()
 
-    def ids_copy(i):
-        return remote(ids_ref, idb.at[c], d2s.at[i], d2r.at[i], cpeer(i))
-
-    vec_y = [remote(vec_ref, vb.at[y], vs.at[i], vr.at[i], ctx(y + i + 1, z)) for i in range(3)]
-    for k in vec_y:
-        k.start()
     ar[pl.ds(e, 1)] = og[pl.ds(e, 1)]
-    vb[pl.ds(y, 1)] = vec_ref[...].reshape(1, 8, 512)
-    idb[pl.ds(c, 1)] = ids_ref[...].reshape(1, 8, 128)
 
     for t in range(TOK):
-        bexp[t] = jnp.broadcast_to(small_ref[0:16, t : t + 1], (16, 128))
+        bexp[t] = jnp.broadcast_to(b_rows[:, t : t + 1], (16, 128))
     cf = c_ref[...]
     c_hi = cf.astype(BF16)
     c_lo = (cf - c_hi.astype(F32)).astype(BF16)
     rep = jnp.where(iota((16, 256), 0) == iota((16, 256), 1) % 16, 1.0, 0.0).astype(BF16)
     keep = (iota((TOK, 256), 1) // 16) == (iota((TOK, 256), 0) % 16)
-    t_hi = jnp.where(keep, dot(c_hi, rep), 0.0).astype(BF16).reshape(8, 16, 256)
-    t_lo = jnp.where(keep, dot(c_lo, rep), 0.0).astype(BF16).reshape(8, 16, 256)
+    t_hi = jnp.where(keep, dot_l(c_hi, rep), 0.0).astype(BF16).reshape(8, 16, 256)
+    t_lo = jnp.where(keep, dot_l(c_lo, rep), 0.0).astype(BF16).reshape(8, 16, 256)
     cbd[:, 0:16, :] = t_hi
     cbd[:, 16:32, :] = t_lo
 
@@ -186,42 +259,10 @@
     macc[...] = jnp.zeros_like(macc)
     zs[...] = jnp.zeros_like(zs)
 
-    def zstep(buf, ss, rr_, s, half):
-        bp = (z - (s - 1) + NZ) % NZ
-        bm = (z + (s - 1)) % NZ
-        if s < 4:
-            return (
-                remote(buf.at[bp], buf.at[bp], ss.at[0, s - 1], rr_.at[0, s - 1], ctx(y, z + 1)),
-                remote(buf.at[bm], buf.at[bm], ss.at[1, s - 1], rr_.at[1, s - 1], ctx(y, z - 1)),
-            )
-        p = buf.at[bp, 0:half]
-        m = buf.at[bm, half : 2 * half]
-        return (
-            remote(p, p, ss.at[0, s - 1], rr_.at[0, s - 1], ctx(y, z + 1)),
-            remote(m, m, ss.at[1, s - 1], rr_.at[1, s - 1], ctx(y, z - 1)),
-        )
-
-    kv_step = [None] + [zstep(kb, zks, zkr, s, NY // 2) for s in range(1, 5)]
-    row_step = [None] + [zstep(rb, rs, rr, s, ROWS) for s in range(1, 5)]
-
-    def start(pair):
-        for q in pair:
-            q.start()
-
-    def wait(pair):
-        for q in pair:
-            q.wait()
-
-    w1 = (
-        remote(wb.at[y], wb.at[y], ws.at[0], wr.at[0], ctx(y + 1, z)),
-        remote(wb.at[y], wb.at[y], ws.at[1], wr.at[1], ctx(y - 1, z)),
-    )
-    ym = (y + NY - 1) % NY
-    yp = (y + 1) % NY
-    w2 = (
-        remote(wb.at[ym, 0 : D // 2], wb.at[ym, 0 : D // 2], ws.at[2], wr.at[2], ctx(y + 1, z)),
-        remote(wb.at[yp, D // 2 : D], wb.at[yp, D // 2 : D], ws.at[3], wr.at[3], ctx(y - 1, z)),
-    )
+    wait(kv_y)
+    start(kv_step[1])
+    wait(own_step[1])
+    start(own_step[2])
 
     @pl.loop(1, NE)
     def _(i):
@@ -233,15 +274,8 @@
     pick = jnp.where(src == di * 32 + dl * 16 + ds, 1.0, 0.0).astype(BF16)
     rb[pl.ds(z, 1)] = dot(pick, ar[...].reshape(256, D)).astype(BF16).reshape(1, 2 * ROWS, D)
     start(row_step[1])
-    wait(kv_y)
-    start(kv_step[1])
-    l2.wait()
-    start(w1)
-
-    @pl.loop(1, NCTX)
-    def _(i):
-        ids_copy(i).start()
-
+    wait(own_step[2])
+    start(own_step[3])
     rim_copy.wait()
 
     @pl.loop(0, NBLK)
@@ -252,11 +286,11 @@
         ext[8 : 8 + TOK, :] = x_ref[:, cols].astype(F32)
         for r in range(0, TOK, 32):
             rows = slice(r, r + 32)
-            s = chan_ref[4:5, cols]
+            s = cbias_ref[0:1, cols]
             for j in range(KCONV):
-                s = s + chan_ref[j : j + 1, cols] * ext[r + 5 + j : r + 37 + j, :]
+                s = s + taps_ref[j : j + 1, cols] * ext[r + 5 + j : r + 37 + j, :]
             cv = s / (1.0 + jnp.exp(-s))
-            raw = dtraw_ref[rows, cols].astype(F32) + chan_ref[5:6, cols]
+            raw = dtraw_ref[rows, cols].astype(F32) + dbias_ref[0:1, cols]
             step = jnp.maximum(raw, 0.0) + jnp.log1p(jnp.exp(-jnp.abs(raw)))
             cvs[rows, cols] = cv
             dts[rows, cols] = step
@@ -294,8 +328,10 @@
 
     pr[pl.ds(c, 1)] = pe[pl.ds(c, 1)]
 
+    start(w1(2))
+
     def attend(zz):
-        key_pos = ((iota((TOK, 512), 1) // TOK) * NZ + zz) * TOK + iota((TOK, 512), 1) % TOK
+        key_pos = (((iota((TOK, 512), 1) // TOK + y) % NY) * NZ + zz) * TOK + iota((TOK, 512), 1) % TOK
         allowed = key_pos <= c * TOK + iota((TOK, 512), 0)
         bias = jnp.where(allowed, 0.0, NEG)
 
@@ -317,6 +353,14 @@
             ms[g] = m_new
 
     attend(z)
+    wait(own_step[3])
+    start(own_step[4])
+    wait(row_step[1])
+    start(row_step[2])
+    wait(kv_step[1])
+    start(kv_step[2])
+    attend((z + 1) % NZ)
+    attend((z + NZ - 1) % NZ)
 
     @pl.loop(1, NCTX)
     def _(i):
@@ -340,17 +384,19 @@
 
     ir[pl.ds(c, 1)] = ic[pl.ds(c, 1)]
 
-    wait(row_step[1])
-    start(row_step[2])
-    wait(kv_step[1])
-    start(kv_step[2])
-
-    attend((z + 1) % NZ)
-    attend((z + NZ - 1) % NZ)
-
-    @pl.loop(1, NCTX)
-    def _(i):
-        inc_copy(i).wait()
+    start(w1(3))
+
+    @pl.loop(1, NCTX)
+    def _(i):
+        ids_copy(i).wait()
+
+    @pl.loop(0, NCTX)
+    def _(i):
+        row = idb[i][0:1, :]
+        lot[pl.ds(i, 1)] = (
+            jnp.where(jnp.bitwise_and(row, 127) == iota((128, 128), 0), 1.0, 0.0)
+            .astype(BF16).reshape(1, 128, 128)
+        )
 
     def second(lo, hi):
         @pl.loop(lo, hi)
@@ -370,67 +416,56 @@
                     h = decay * h + b * u16[tt : tt + 1, :]
                     hb[16 * tt : 16 * tt + 16, :] = h.astype(BF16)
                 both = dot(cbd[g], hb[...])
-                out = both[0:16, :] + both[16:32, :] + chan_ref[6:7, cols] * cvs[rows, cols]
+                out = both[0:16, :] + both[16:32, :] + skip_ref[0:1, cols] * cvs[rows, cols]
                 zg = z_ref[rows, cols].astype(F32)
                 out = (out * (zg / (1.0 + jnp.exp(-zg)))).astype(BF16).astype(F32)
-                macc[rows, :] += lane_sum(out * chan_ref[7:8, cols])
+                macc[rows, :] += lane_sum(out * mvec_ref[0:1, cols])
                 return h
 
             lax.fori_loop(0, TOK // 16, group, h0)
-
-    second(0, NBLK // 2)
-    wait(row_step[2])
-    start(row_step[3])
-    second(NBLK // 2, NBLK)
-    wait(kv_step[2])
-    start(kv_step[3])
-    attend((z + 2) % NZ)
-    attend((z + NZ - 2) % NZ)
-
-    wait(row_step[3])
-    start(row_step[4])
-
-    @pl.loop(1, NCTX)
-    def _(i):
-        ids_copy(i).wait()
-
-    @pl.loop(0, NCTX)
-    def _(i):
-        row = idb[i][0:1, :]
-        lot[pl.ds(i, 1)] = (
-            jnp.where(jnp.bitwise_and(row, 127) == iota((128, 128), 0), 1.0, 0.0)
-            .astype(BF16).reshape(1, 128, 128)
-        )
-
-    wait(w1)
-    start(w2)
-    wait(vec_y)
-    wait(row_step[4])
 
     def experts(yb):
         for l in range(2):
             rows = rb[:, l * ROWS : (l + 1) * ROWS, :].reshape(NZ * ROWS, D)
-            part = wb[pl.ds(yb, 1), :, l * 384 : l * 384 + 512].reshape(D, 512)
-            both = dot(rows, part)
-            up = pltpu.roll(both, 512 - FFL, 1)
-            inner = ((both / (1.0 + jnp.exp(-both))) * up).astype(BF16).astype(F32)
-            vec = vb[pl.ds(yb, 1)].reshape(8, 512)[l : l + 1, :]
-            ma[l] += lane_sum(inner * vec)
-
-    @pl.loop(0, 3)
-    def _(i):
-        experts((y + jnp.where(i == 2, NY - 1, i)) % NY)
-
+            gate = dot_t(rows, wb[pl.ds(yb, 1), 2 * l * FFL : (2 * l + 1) * FFL, :].reshape(FFL, D))
+            up = dot_t(rows, wb[pl.ds(yb, 1), (2 * l + 1) * FFL : (2 * l + 2) * FFL, :].reshape(FFL, D))
+            inner = ((gate / (1.0 + jnp.exp(-gate))) * up).astype(BF16).astype(F32)
+            term = inner * vb[pl.ds(yb, 1)].reshape(8, FFL)[l : l + 1, :]
+            ma[l] += jnp.sum(term, axis=1, keepdims=True)
+
+    wait(row_step[2])
+    start(row_step[3])
+    wait(kv_step[2])
+    start(kv_step[3])
+    for q in range(4):
+        wait(w1(q))
+    start(w2)
+    @pl.loop(1, NCTX)
+    def _(i):
+        inc_copy(i).wait()
+
+    second(0, NBLK // 2)
+    wait(row_step[3])
+    start(row_step[4])
+    second(NBLK // 2, NBLK)
+    attend((z + 2) % NZ)
+    attend((z + NZ - 2) % NZ)
     wait(kv_step[3])
     start(kv_step[4])
+    wait(vec_y)
+    wait(row_step[4])
+
+    @pl.loop(0, 3)
+    def _(i):
+        experts((y + jnp.where(i == 2, NY - 1, i)) % NY)
+
     attend((z + 3) % NZ)
     attend((z + NZ - 3) % NZ)
-
     wait(w2)
     experts((y + 2) % NY)
 
     for l in range(2):
-        col = jnp.sum(ma[l], axis=1, keepdims=True)
+        col = ma[l][:, 0:1]
         for q in range(NZ):
             zs[q, l : l + 1, :] = to_row(col[q * ROWS : (q + 1) * ROWS, :])
 
@@ -442,6 +477,7 @@
         z_copy(i).start()
 
     zr[pl.ds(z, 1)] = zs[pl.ds(z, 1)]
+    wait(own_step[4])
     wait(kv_step[4])
     attend((z + 4) % NZ)
 
@@ -471,11 +507,11 @@
         ratio = (acc[g] / ls[g]).astype(BF16).astype(F32)
         for j in range(GROUPS):
             h = g * GROUPS + j
-            attn = attn + ratio[j * TOK : (j + 1) * TOK, :] * feat_ref[0:1, h * HD : (h + 1) * HD]
+            attn = attn + ratio[j * TOK : (j + 1) * TOK, :] * avec_ref[0:1, h * HD : (h + 1) * HD]
     attn_col = jnp.sum(attn, axis=1, keepdims=True)
     mamba_col = jnp.sum(macc[...], axis=1, keepdims=True)
     own = to_row(base_s[:, 0:1] + attn_col + mamba_col)
-    id_row = ids_ref[0:1, :].astype(F32)
+    id_row = terms_ref[...].astype(F32)
     id_same = to_col(id_row) == id_row
     chosen, before, gates = routing()
 
@@ -491,7 +527,7 @@
         one = jnp.sum(jnp.where(iota((16, 128), 1) == e * CAP + s, back, 0.0), axis=1, keepdims=True)
         value = value + jnp.where((chosen == 1.0) & (before == float(s)), one, 0.0)
     expert = jnp.sum(value * gates, axis=0, keepdims=True)
-    impacts = small_ref[20:21, :] * jnp.maximum(own + expert, 0.0)
+    impacts = live * jnp.maximum(own + expert, 0.0)
     imp_ref[...] = impacts
 
     imp_col = to_col(impacts)
@@ -499,7 +535,7 @@
     beaten = id_same & ((imp_col > impacts) | ((imp_col == impacts) & earlier))
     beaten = jnp.max(jnp.where(beaten, 1.0, 0.0), axis=0, keepdims=True)
     sent = jnp.where(beaten > 0.0, 0.0, impacts)
-    imps[pl.ds(c, 1)] = jnp.broadcast_to(sent, (8, 128)).reshape(1, 8, 128)
+    imps[pl.ds(c, 1)] = sent.reshape(1, 1, 128)
 
     def imp_copy(i):
         return remote(imps.at[c], imps.at[c], i2s.at[i], i2r.at[i], cpeer(i))
@@ -532,36 +568,19 @@
     dt_bias, a_rate, skip_gain, mamba_vector, attn_vector, impact_vector, norm_gain, expert_gate,
     expert_up, expert_vector, routes, route_gate, lengths, term_ids,
 ):
-    e = lax.axis_index("expert")
-    c = lax.axis_index("context")
-    length = lax.dynamic_index_in_dim(lengths, e, 0, False)
-    live = (c * TOK + jnp.arange(TOK, dtype=jnp.int32) < length).astype(F32)
-    small = jnp.concatenate(
-        [b_proj[0].T, routes[0].T.astype(F32), route_gate[0].T, live[None, :], jnp.zeros((3, TOK), F32)],
-        axis=0,
-    )
-    ids = jnp.broadcast_to(term_ids, (8, TOK))
-    chan = jnp.concatenate(
-        [conv_weight, conv_bias[None], dt_bias[None], skip_gain[None], mamba_vector[None]], axis=0
-    )
-    feat = jnp.stack([attn_vector, impact_vector, norm_gain, norm_gain])
-    weights = jnp.concatenate([expert_gate[0], expert_up[0], expert_gate[1], expert_up[1]], axis=1)
-    vec = jnp.concatenate(
-        [jnp.pad(expert_vector[0:1], ((0, 0), (0, 512 - FFL))),
-         jnp.pad(expert_vector[1:2], ((0, 0), (64, 512 - FFL - 64))),
-         jnp.zeros((6, 512), F32)],
-        axis=0,
-    )
     dma = pltpu.SemaphoreType.DMA
     vmem = pltpu.VMEM
     outs = pl.pallas_call(
         kernel,
         name="layers",
         out_shape=OUT_SHAPE,
-        in_specs=[pl.BlockSpec(memory_space=pltpu.VMEM)] * 14 + [pl.BlockSpec(memory_space=pl.ANY)],
+        in_specs=[pl.BlockSpec(memory_space=pltpu.VMEM)] * 12
+        + [pl.BlockSpec(memory_space=pltpu.SMEM)]
+        + [pl.BlockSpec(memory_space=pltpu.VMEM)] * 10
+        + [pl.BlockSpec(memory_space=pl.ANY)] * 2,
         out_specs=OUT_SPECS,
         scratch_shapes=[
-            vmem((NY, D, 4 * FFL), BF16), vmem((NZ, NY, TOK, 1024), BF16), vmem((NZ, 2 * ROWS, D), BF16),
+            vmem((NY, 4 * FFL, D), BF16), vmem((NZ, NY, TOK, 1024), BF16), vmem((NZ, 2 * ROWS, D), BF16),
             vmem((NE, 32, D), BF16), vmem((NE, 32, D), BF16),
             vmem((TOK, INNER), F32), vmem((TOK, INNER), F32), vmem((TOK, INNER), F32),
             vmem((8 + TOK, BLK), F32), vmem((16, INNER), BF16), vmem((TOK, 16, 128), F32),
@@ -570,13 +589,13 @@
             vmem((NCTX, 16, 128), F32), vmem((NCTX, 16, 128), F32),
             vmem((KVH, GROUPS * TOK, HD), BF16), vmem((KVH, GROUPS * TOK, HD), F32),
             vmem((KVH, GROUPS * TOK, 128), F32), vmem((KVH, GROUPS * TOK, 128), F32),
-            vmem((NY, 8, 512), F32), vmem((2, NZ * ROWS, 128), F32),
+            vmem((NY, 8, FFL), F32), vmem((2, NZ * ROWS, 128), F32),
             vmem((NZ, 8, 128), F32), vmem((NZ, 8, 128), F32),
             vmem((16, 128), F32), vmem((NE, 16, 128), F32),
-            vmem((NCTX, 8, 128), F32), vmem((NCTX, 8, 128), jnp.int32), vmem((NCTX, 128, 128), BF16),
+            vmem((NCTX, 1, 128), F32), vmem((NCTX, 1, 128), jnp.int32), vmem((NCTX, 128, 128), BF16),
             vmem((TOK, 128), F32), vmem((TOK, 128), F32),
-            dma((3,)), dma((4,)), dma((4,)), dma((3,)), dma((3,)), dma((3,)), dma((3,)),
-            dma((2, 4)), dma((2, 4)), dma((2, 4)), dma((2, 4)), dma((NE,)), dma((NE,)), dma, dma,
+            dma((6,)), dma((2, 5)), dma((2, 5)), dma((3,)), dma((3,)), dma((3,)), dma((3,)),
+            dma((2, 4)), dma((2, 4)), dma((2, 4)), dma((2, 4)), dma((2, 4)), dma((2, 4)), dma((NE,)), dma((NE,)), dma, dma,
             dma((NCTX,)), dma((NCTX,)), dma((NCTX,)), dma((NCTX,)),
             dma((NZ,)), dma((NZ,)), dma((NE,)), dma((NE,)), dma((NCTX,)), dma((NCTX,)),
             dma((NCTX,)), dma((NCTX,)),
@@ -585,8 +604,10 @@
             collective_id=0, has_side_effects=True, vmem_limit_bytes=VMEM_LIMIT
         ),
     )(
-        hidden[0], query[0], keys[0], values[0], x_inner[0], z_gate[0], dt_raw[0], c_proj[0], a_rate,
-        small, ids, chan, feat, vec, weights,
+        hidden[0], query[0], keys[0], values[0], x_inner[0], z_gate[0], dt_raw[0], c_proj[0].T, a_rate,
+        b_proj[0].T, routes[0].T, route_gate[0].T, lengths, term_ids, conv_weight, conv_bias[None],
+        dt_bias[None], skip_gain[None], mamba_vector[None], attn_vector[None], impact_vector[None],
+        norm_gain[None], expert_vector, jnp.swapaxes(expert_gate, 1, 2), jnp.swapaxes(expert_up, 1, 2),
     )
     return tuple(outs)
 

time: 275 us -> 207 us (0.75)
  Pallas kernels: 247 us -> 203 us
  local copies, waits for them, and re-layouts: 18.3 us -> 2.43 us
  other arithmetic: 7.91 us -> 0 us
    pallas_call x1, Pallas kernels: 247 us -> 203 us  [shards(): pl.pallas_call(kernel, name='layers', out_shape=OUT_SHAPE, in_specs=[pl.B...]
    concatenate x2 -> x0, other arithmetic: 5.94 us -> none  [the longest x1 5.26 us: shards(): jnp.concatenate([expert_gate[0], expert_up[0], expert_gate[1], expert_up[...]
    unnamed x29 -> x2, local copies, waits for them, and re-layouts: 7.93 us -> 2.43 us
    slice x3 -> x0, local copies, waits for them, and re-layouts: 5.18 us -> none  [the longest x1 2.62 us: shards(): expert_gate[0]]
    concatenate x3 -> x0, local copies, waits for them, and re-layouts: 3.4 us -> none  [the longest x1 2.56 us: shards(): jnp.concatenate([b_proj[0].T, routes[0].T.astype(F32), route_gate[0].T, l...]
where the time goes in v2:
time: 207 us; the launch traced here: 206 us
  Pallas kernels  203 us (98%)
  local copies, waits for them, and re-layouts  2.43 us (1%)
    pallas_call x1, Pallas kernels, shards(): pl.pallas_call(kernel, name='layers', out_shape=OUT_SHAPE, in_specs=[pl.B...  203 us

profile of v2, /device:TPU:1, one launch (start us, length us, event | category | flops | bytes accessed | tf_op | source)
XLA Modules:
  0.0 206.4 jit_solution(18298132285488381606)
XLA Ops:
  0.6 203.3 %layers.1 = (f32[1,128]{1,0:T(1,128)}, f32[1,2048]{1,0:T(1,128)}) custom-call(bf16[128,2048]{1,0:T(8,128)(2,1)} %bitcast.33, bf16[128,2048]{1,0:T(8,128)(2,1)} %bitcast.34, bf16[128,512]{1,0:T(8,128)(2,1)} %bitcast.35, bf16[128,512]{1,0:T(8,128)(2,1)} %bitcast.36, bf16[128,4096]{1,0:T(8,128)(2,1)} %bitcast.30, bf16[128,4096]{1,0:T(8,128)(2,1)} %bitcast.31, ...), custom_call_target="tpu_custom_call" | custom-call | tf_op jit(solution)/shard_map/layers/pallas_call | solution.py:573
  204.0 1.1 copy.29
  205.1 1.3 copy.30

commit v3 on v2

--- a/solution.py
+++ b/solution.py
@@ -236,6 +236,9 @@
 
     ar[pl.ds(e, 1)] = og[pl.ds(e, 1)]
 
+    wait(own_step[1])
+    start(own_step[2])
+
     for t in range(TOK):
         bexp[t] = jnp.broadcast_to(b_rows[:, t : t + 1], (16, 128))
     cf = c_ref[...]
@@ -259,11 +262,6 @@
     macc[...] = jnp.zeros_like(macc)
     zs[...] = jnp.zeros_like(zs)
 
-    wait(kv_y)
-    start(kv_step[1])
-    wait(own_step[1])
-    start(own_step[2])
-
     @pl.loop(1, NE)
     def _(i):
         a2a(i).wait()
@@ -274,50 +272,60 @@
     pick = jnp.where(src == di * 32 + dl * 16 + ds, 1.0, 0.0).astype(BF16)
     rb[pl.ds(z, 1)] = dot(pick, ar[...].reshape(256, D)).astype(BF16).reshape(1, 2 * ROWS, D)
     start(row_step[1])
+    wait(kv_y)
+    start(kv_step[1])
+    rim_copy.wait()
+
+    def first(lo, hi):
+        @pl.loop(lo, hi)
+        def _(k):
+            cols = pl.ds(pl.multiple_of(k * BLK, BLK), BLK)
+            edge = jnp.where(c == 0, 0.0, rim[:, cols].astype(F32))
+            ext[0:8, :] = edge[8:16, :]
+            ext[8 : 8 + TOK, :] = x_ref[:, cols].astype(F32)
+            for r in range(0, TOK, 32):
+                rows = slice(r, r + 32)
+                s = cbias_ref[0:1, cols]
+                for j in range(KCONV):
+                    s = s + taps_ref[j : j + 1, cols] * ext[r + 5 + j : r + 37 + j, :]
+                cv = s / (1.0 + jnp.exp(-s))
+                raw = dtraw_ref[rows, cols].astype(F32) + dbias_ref[0:1, cols]
+                step = jnp.maximum(raw, 0.0) + jnp.log1p(jnp.exp(-jnp.abs(raw)))
+                cvs[rows, cols] = cv
+                dts[rows, cols] = step
+                us[rows, cols] = step * cv
+            a2 = a_ref[:, cols] * (-LOG2E)
+
+            def group(g, carried):
+                h, total = carried
+                base = pl.multiple_of(g * 16, 16)
+                d16 = dts[pl.ds(base, 16), cols]
+                u16 = us[pl.ds(base, 16), cols]
+                for tt in range(16):
+                    b = jnp.concatenate([bexp[base + tt]] * (BLK // 128), axis=1)
+                    decay = jnp.exp2(a2 * d16[tt : tt + 1, :])
+                    h = decay * h + b * u16[tt : tt + 1, :]
+                return h, total + jnp.sum(d16, axis=0, keepdims=True)
+
+            h, total = lax.fori_loop(
+                0, TOK // 16, group, (jnp.zeros((NSTATE, BLK), F32), jnp.zeros((1, BLK), F32))
+            )
+            t0 = total.astype(BF16).astype(F32)
+            t1 = (total - t0).astype(BF16).astype(F32)
+            which = iota((16, BLK), 0)
+            total_rows = jnp.where(which == 0, t0, jnp.where(which == 1, t1, total - t0 - t1))
+            for i in range(BLK // 128):
+                part = jnp.concatenate(
+                    [h[:, 128 * i : 128 * i + 128],
+                     total_rows[:, 128 * i : 128 * i + 128]],
+                    axis=0,
+                )
+                pe[pl.ds(k * (BLK // 128) + i, 1)] = part.astype(BF16).reshape(1, 32, 128)
+
+    first(0, NBLK // 2)
     wait(own_step[2])
     start(own_step[3])
-    rim_copy.wait()
-
-    @pl.loop(0, NBLK)
-    def _(k):
-        cols = pl.ds(pl.multiple_of(k * BLK, BLK), BLK)
-        edge = jnp.where(c == 0, 0.0, rim[:, cols].astype(F32))
-        ext[0:8, :] = edge[8:16, :]
-        ext[8 : 8 + TOK, :] = x_ref[:, cols].astype(F32)
-        for r in range(0, TOK, 32):
-            rows = slice(r, r + 32)
-            s = cbias_ref[0:1, cols]
-            for j in range(KCONV):
-                s = s + taps_ref[j : j + 1, cols] * ext[r + 5 + j : r + 37 + j, :]
-            cv = s / (1.0 + jnp.exp(-s))
-            raw = dtraw_ref[rows, cols].astype(F32) + dbias_ref[0:1, cols]
-            step = jnp.maximum(raw, 0.0) + jnp.log1p(jnp.exp(-jnp.abs(raw)))
-            cvs[rows, cols] = cv
-            dts[rows, cols] = step
-            us[rows, cols] = step * cv
-        a2 = a_ref[:, cols] * (-LOG2E)
-
-        def group(g, carried):
-            h, total = carried
-            base = pl.multiple_of(g * 16, 16)
-            d16 = dts[pl.ds(base, 16), cols]
-            u16 = us[pl.ds(base, 16), cols]
-            for tt in range(16):
-                b = jnp.concatenate([bexp[base + tt]] * (BLK // 128), axis=1)
-                decay = jnp.exp2(a2 * d16[tt : tt + 1, :])
-                h = decay * h + b * u16[tt : tt + 1, :]
-            return h, total + jnp.sum(d16, axis=0, keepdims=True)
-
-        h, total = lax.fori_loop(
-            0, TOK // 16, group, (jnp.zeros((NSTATE, BLK), F32), jnp.zeros((1, BLK), F32))
-        )
-        for i in range(BLK // 128):
-            part = jnp.concatenate(
-                [h[:, 128 * i : 128 * i + 128],
-                 jnp.broadcast_to(total[:, 128 * i : 128 * i + 128], (8, 128))],
-                axis=0,
-            )
-            pe[pl.ds(k * (BLK // 128) + i, 1)] = part.reshape(1, 24, 128)
+    first(NBLK // 2, NBLK)
 
     def end_copy(i):
         return remote(pe.at[(c + i) % NCTX], pr.at[c], ps.at[i], prs.at[i], cpeer(i))
@@ -352,13 +360,13 @@
             acc[g] = alpha * acc[g] + dot(p.astype(BF16), vv)
             ms[g] = m_new
 
+    wait(row_step[1])
+    start(row_step[2])
     attend(z)
+    wait(kv_step[1])
+    start(kv_step[2])
     wait(own_step[3])
     start(own_step[4])
-    wait(row_step[1])
-    start(row_step[2])
-    wait(kv_step[1])
-    start(kv_step[2])
     attend((z + 1) % NZ)
     attend((z + NZ - 1) % NZ)
 
@@ -369,9 +377,10 @@
     a2c = a_ref[:, pl.ds(pl.multiple_of(c * 128, 128), 128)] * (-LOG2E)
 
     def join(i, state):
-        ic[pl.ds(i, 1)] = state.reshape(1, NSTATE, 128)
-        part = pr[i]
-        return jnp.exp2(a2c * part[16:17, :]) * state + part[0:16, :]
+        ic[pl.ds(i, 1)] = state.astype(BF16).reshape(1, NSTATE, 128)
+        part = pr[i].astype(F32)
+        gone = (part[16:17, :] + part[17:18, :]) + part[18:19, :]
+        return jnp.exp2(a2c * gone) * state + part[0:16, :]
 
     lax.fori_loop(0, NCTX, join, jnp.zeros((NSTATE, 128), F32))
 
@@ -403,7 +412,7 @@
         def _(k):
             cols = pl.ds(pl.multiple_of(k * BLK, BLK), BLK)
             a2 = a_ref[:, cols] * (-LOG2E)
-            h0 = jnp.concatenate([ir[k * (BLK // 128) + i] for i in range(BLK // 128)], axis=1)
+            h0 = jnp.concatenate([ir[k * (BLK // 128) + i] for i in range(BLK // 128)], axis=1).astype(F32)
 
             def group(g, h):
                 base = pl.multiple_of(g * 16, 16)
@@ -437,6 +446,8 @@
     start(row_step[3])
     wait(kv_step[2])
     start(kv_step[3])
+    attend((z + 2) % NZ)
+    attend((z + NZ - 2) % NZ)
     for q in range(4):
         wait(w1(q))
     start(w2)
@@ -448,10 +459,10 @@
     wait(row_step[3])
     start(row_step[4])
     second(NBLK // 2, NBLK)
-    attend((z + 2) % NZ)
-    attend((z + NZ - 2) % NZ)
     wait(kv_step[3])
     start(kv_step[4])
+    attend((z + 3) % NZ)
+    attend((z + NZ - 3) % NZ)
     wait(vec_y)
     wait(row_step[4])
 
@@ -459,8 +470,9 @@
     def _(i):
         experts((y + jnp.where(i == 2, NY - 1, i)) % NY)
 
-    attend((z + 3) % NZ)
-    attend((z + NZ - 3) % NZ)
+    wait(own_step[4])
+    wait(kv_step[4])
+    attend((z + 4) % NZ)
     wait(w2)
     experts((y + 2) % NY)
 
@@ -477,9 +489,6 @@
         z_copy(i).start()
 
     zr[pl.ds(z, 1)] = zs[pl.ds(z, 1)]
-    wait(own_step[4])
-    wait(kv_step[4])
-    attend((z + 4) % NZ)
 
     @pl.loop(1, NZ)
     def _(i):
@@ -548,7 +557,7 @@
     def _(i):
         imp_copy(i).wait()
 
-    def pool(i, best):
+    def pooled(i):
         word = jnp.right_shift(idb[i][0:1, :], 7) - c * 16
         val = jnp.where(word == iota((16, 128), 0), imps[i][0:1, :], 0.0)
         p0 = val.astype(BF16)
@@ -556,9 +565,15 @@
         p1 = rest.astype(BF16)
         p2 = (rest - p1.astype(F32)).astype(BF16)
         got = dot_t(jnp.concatenate([p0, p1, p2], axis=0), lot[i])
-        return jnp.maximum(best, (got[0:16] + got[16:32]) + got[32:48])
-
-    best = lax.fori_loop(0, NCTX, pool, jnp.zeros((16, 128), F32))
+        return (got[0:16] + got[16:32]) + got[32:48]
+
+    def pool(i, best):
+        quad = [pooled(8 * i + k) for k in range(8)]
+        while len(quad) > 1:
+            quad = [jnp.maximum(a, b) for a, b in zip(quad[0::2], quad[1::2])]
+        return jnp.maximum(best, quad[0])
+
+    best = lax.fori_loop(0, NCTX // 8, pool, jnp.zeros((16, 128), F32))
     for r in range(16):
         term_ref[0:1, 128 * r : 128 * r + 128] = best[r : r + 1, :]
 
@@ -585,8 +600,8 @@
             vmem((TOK, INNER), F32), vmem((TOK, INNER), F32), vmem((TOK, INNER), F32),
             vmem((8 + TOK, BLK), F32), vmem((16, INNER), BF16), vmem((TOK, 16, 128), F32),
             vmem((8, 32, 256), BF16), vmem((256, BLK), BF16),
-            vmem((NCTX, 24, 128), F32), vmem((NCTX, 24, 128), F32),
-            vmem((NCTX, 16, 128), F32), vmem((NCTX, 16, 128), F32),
+            vmem((NCTX, 32, 128), BF16), vmem((NCTX, 32, 128), BF16),
+            vmem((NCTX, 16, 128), BF16), vmem((NCTX, 16, 128), BF16),
             vmem((KVH, GROUPS * TOK, HD), BF16), vmem((KVH, GROUPS * TOK, HD), F32),
             vmem((KVH, GROUPS * TOK, 128), F32), vmem((KVH, GROUPS * TOK, 128), F32),
             vmem((NY, 8, FFL), F32), vmem((2, NZ * ROWS, 128), F32),

time: 207 us -> 186 us (0.90)
  Pallas kernels: 203 us -> 183 us
    pallas_call x1, Pallas kernels: 203 us -> 183 us  [shards(): pl.pallas_call(kernel, name='layers', out_shape=OUT_SHAPE, in_specs=[pl.B...]
where the time goes in v3:
time: 186 us
  Pallas kernels  183 us (98%)
  local copies, waits for them, and re-layouts  2.43 us (1%)
    pallas_call x1, Pallas kernels, shards(): pl.pallas_call(kernel, name='layers', out_shape=OUT_SHAPE, in_specs=[pl.B...  183 us

profile of v3, /device:TPU:1, one launch (start us, length us, event | category | flops | bytes accessed | tf_op | source)
XLA Modules:
  0.0 186.1 jit_solution(18141777337167230448)
XLA Ops:
  0.6 183.0 %layers.1 = (f32[1,128]{1,0:T(1,128)}, f32[1,2048]{1,0:T(1,128)}) custom-call(bf16[128,2048]{1,0:T(8,128)(2,1)} %bitcast.33, bf16[128,2048]{1,0:T(8,128)(2,1)} %bitcast.34, bf16[128,512]{1,0:T(8,128)(2,1)} %bitcast.35, bf16[128,512]{1,0:T(8,128)(2,1)} %bitcast.36, bf16[128,4096]{1,0:T(8,128)(2,1)} %bitcast.30, bf16[128,4096]{1,0:T(8,128)(2,1)} %bitcast.31, ...), custom_call_target="tpu_custom_call" | custom-call | tf_op jit(solution)/shard_map/layers/pallas_call | solution.py:588
  183.6 1.1 copy.29
  184.8 1.3 copy.30

commit v4 on v3

--- a/solution.py
+++ b/solution.py
@@ -470,9 +470,6 @@
     def _(i):
         experts((y + jnp.where(i == 2, NY - 1, i)) % NY)
 
-    wait(own_step[4])
-    wait(kv_step[4])
-    attend((z + 4) % NZ)
     wait(w2)
     experts((y + 2) % NY)
 
@@ -489,6 +486,9 @@
         z_copy(i).start()
 
     zr[pl.ds(z, 1)] = zs[pl.ds(z, 1)]
+    wait(own_step[4])
+    wait(kv_step[4])
+    attend((z + 4) % NZ)
 
     @pl.loop(1, NZ)
     def _(i):

time: 186 us -> 184 us (0.989)
  Pallas kernels: 183 us -> 181 us
    pallas_call x1, Pallas kernels: 183 us -> 181 us  [shards(): pl.pallas_call(kernel, name='layers', out_shape=OUT_SHAPE, in_specs=[pl.B...]
where the time goes in v4:
time: 184 us
  Pallas kernels  181 us (98%)
  local copies, waits for them, and re-layouts  2.43 us (1%)
    pallas_call x1, Pallas kernels, shards(): pl.pallas_call(kernel, name='layers', out_shape=OUT_SHAPE, in_specs=[pl.B...  181 us

profile of v4, /device:TPU:1, one launch (start us, length us, event | category | flops | bytes accessed | tf_op | source)
XLA Modules:
  0.0 183.6 jit_solution(2253314097661812117)
XLA Ops:
  0.6 180.5 %layers.1 = (f32[1,128]{1,0:T(1,128)}, f32[1,2048]{1,0:T(1,128)}) custom-call(bf16[128,2048]{1,0:T(8,128)(2,1)} %bitcast.33, bf16[128,2048]{1,0:T(8,128)(2,1)} %bitcast.34, bf16[128,512]{1,0:T(8,128)(2,1)} %bitcast.35, bf16[128,512]{1,0:T(8,128)(2,1)} %bitcast.36, bf16[128,4096]{1,0:T(8,128)(2,1)} %bitcast.30, bf16[128,4096]{1,0:T(8,128)(2,1)} %bitcast.31, ...), custom_call_target="tpu_custom_call" | custom-call | tf_op jit(solution)/shard_map/layers/pallas_call | solution.py:588
  181.2 1.1 copy.29
  182.3 1.3 copy.30
